TPU v7x, 128 devices: a whole 4x4x4 slice. The times are simulated.
128 devices in a mesh: feat: 64 (over x, y, z_lo, core), rows: 2 (over z_hi).
Axes of the slice: x: 4, y: 4, z: 4 (z_hi: 2, z_lo: 2; z = z_hi * 2 + z_lo), core: 2. Of those that a mesh axis runs over, the one named last changes fastest.
Arguments:
- embeddings: bfloat16 [256, 512], P('rows'), may hold values from -6 to 6
- sign_flips: float32 [524288], P('feat'), may hold values from -1 to 1, as said below
- gaussian: float32 [524288], P('feat'), may hold values from -5 to 5
- scales: float32 [524288], P('feat'), may hold values from 0.5 to 2
- phases: float32 [524288], P('feat'), may hold values from 0 to 6.2831855
- source_blocks: int32 [4096], P('feat'), may hold values from 0 to 4095, as said below
- block_permutations: bfloat16 [4096, 128, 128], P('feat'), may hold values from 0 to 1, as said below
- weights: float32 [524288], P('feat'), may hold values from -6 to 6
- targets: float32 [256], P('rows'), may hold values from -6 to 6
Outputs:
- predictions: float32 [256], P('rows')
- feature_grad: float32 [524288], P(('feat', 'rows'))
Inputs may be any that keep to these rules, and one draw needn't show every extreme that they name: `sign_flips`: each entry is -1 or 1. `source_blocks`: A permutation of the 4096 block numbers. The 64 entries of each aligned run of 64 entries name exactly 1 block from every aligned run of 64 blocks. Each block_permutations[b] is a permutation matrix.
All inputs are finite; a program needn't handle non-finite values.
Results may differ from a plain program's by a relative error of at most 0.0003.
Values sent between devices are 32-bit elements; how exact they have to be, the bound alone decides.
A program may use at most 64 MiB of HBM per device.

v0:
```python
import math

import jax
import jax.numpy as jnp
from jax import lax
from jax.sharding import PartitionSpec as P

FEATURE_COUNT = 524288


def rademacher_signs(length):
    indices = jnp.arange(length, dtype=jnp.int32)
    joined = jnp.bitwise_and(indices[:, None], indices[None, :])
    parity = jnp.zeros((length, length), jnp.int32)
    for bit_number in range(length.bit_length() - 1):
        parity = parity + jnp.bitwise_and(jnp.right_shift(joined, bit_number), 1)
    return (1 - 2 * jnp.bitwise_and(parity, 1)).astype(jnp.float32)


def transform(field, block):
    row_count = field.shape[0]
    feat_here = field.shape[1]
    outer = feat_here // block
    values = field.reshape(row_count, outer, block)
    values = jnp.einsum(
        "rac,dc->rad", values, rademacher_signs(block), precision=lax.Precision.HIGHEST
    )
    values = jnp.einsum(
        "rac,ba->rbc", values, rademacher_signs(outer), precision=lax.Precision.HIGHEST
    )
    device_shards = lax.axis_size("feat")
    spread = values
    across_devices = lax.all_to_all(spread, "feat", split_axis=1, concat_axis=1, tiled=True)
    combined = jnp.einsum(
        "gwf,aw->gaf",
        across_devices,
        rademacher_signs(device_shards),
        precision=lax.Precision.HIGHEST,
    )
    returned = lax.all_to_all(combined, "feat", split_axis=1, concat_axis=1, tiled=True)
    values = returned.reshape(row_count, feat_here)
    return values * (1.0 / math.sqrt(FEATURE_COUNT))


def local(
    embeddings,
    sign_flips,
    gaussian,
    scales,
    phases,
    source_blocks,
    block_permutations,
    weights,
    targets,
):
    row_count = embeddings.shape[0]
    width = embeddings.shape[1]
    feat_here = sign_flips.shape[0]
    blk_here = block_permutations.shape[0]
    block = block_permutations.shape[1]
    device_shards = lax.axis_size("feat")
    per_pair = blk_here // device_shards
    tiled = jnp.tile(embeddings.astype(jnp.float32), (1, feat_here // width)) * sign_flips[None, :]
    first = transform(tiled, block)
    source_dev = source_blocks // blk_here
    source_local = source_blocks % blk_here
    slot_keys = source_dev * blk_here + jnp.arange(blk_here, dtype=jnp.int32)
    ordering = jnp.argsort(slot_keys)
    inverse = jnp.argsort(ordering)
    wanted = jnp.take(source_local, ordering).reshape(device_shards, per_pair)
    asked = lax.all_to_all(wanted, "feat", split_axis=0, concat_axis=0, tiled=True)
    first_blocks = first.reshape(row_count, blk_here, block)
    outgoing = jnp.take(first_blocks, asked.reshape(-1), axis=1)
    incoming = lax.all_to_all(outgoing, "feat", split_axis=1, concat_axis=1, tiled=True)
    placed = jnp.take(incoming, inverse, axis=1)
    mixed = jnp.einsum(
        "rbj,bij->rbi",
        placed,
        block_permutations.astype(jnp.float32),
        precision=lax.Precision.HIGHEST,
    )
    mixed = mixed.reshape(row_count, feat_here) * gaussian[None, :]
    second = transform(mixed, block)
    features = jnp.cos(scales[None, :] * second + phases[None, :])
    local_sum = jnp.dot(features, weights, precision=lax.Precision.HIGHEST)
    predictions = lax.psum(local_sum, "feat") * (1.0 / math.sqrt(FEATURE_COUNT))
    residual = predictions - targets
    total_rows = row_count * lax.axis_size("rows")
    grad_terms = jnp.dot(residual, features, precision=lax.Precision.HIGHEST) * (
        1.0 / math.sqrt(total_rows)
    )
    feature_grad = lax.psum_scatter(grad_terms, "rows", scatter_dimension=0, tiled=True)
    return (predictions, feature_grad)


def solution(mesh):
    in_specs = (
        P("rows", None),
        P("feat"),
        P("feat"),
        P("feat"),
        P("feat"),
        P("feat"),
        P("feat", None, None),
        P("feat"),
        P("rows"),
    )
    out_specs = (P("rows"), P(("feat", "rows")))
    return jax.shard_map(local, mesh=mesh, in_specs=in_specs, out_specs=out_specs, check_vma=False)
```

profile of v0, /device:TPU:0, one launch (start us, length us, event | category | flops | bytes accessed | tf_op | source)
XLA Modules:
  0.0 581.3 jit_solution(2201603233594802488)
XLA Ops:
  0.6 3.5 tile.4
  4.2 4.8 tile.10
  8.9 6.5 %fusion.11 = f32[128,64,128]{2,1,0:T(8,128)S(1)} fusion(f32[128,64,128]{2,1,0:T(8,128)} %tile.10, f32[64,128]{1,0:T(8,128)S(1)} %bitcast.56), kind=kOutput, calls=%fused_computation.17 | convolution fusion | flops 1612070912 | bytes 8421376 | tf_op jit(solution)/shard_map/rac,dc->rad/dot_general | solution.py:25
  15.5 3.9 convolution_bitcast_fusion.1
  19.3 4.4 copy.25
  23.7 9.8 %all-to-all-start = ((f32[128,64,128]{2,0,1:T(8,128)}), f32[128,64,128]{2,0,1:T(8,128)}, u32[]{:S(2)}, u32[]{:S(2)}) async-start(f32[128,64,128]{2,0,1:T(8,128)} %copy.25), calls=%async_computation | async-start | bytes 8388608 | tf_op jit(solution)/shard_map/all_to_all | solution.py:33
  37.1 47.5 %all-to-all-done = f32[128,64,128]{2,0,1:T(8,128)} async-done(((f32[128,64,128]{2,0,1:T(8,128)}), f32[128,64,128]{2,0,1:T(8,128)}, u32[]{:S(2)}, u32[]{:S(2)}) %all-to-all-start) | async-done | bytes 4194336 | tf_op jit(solution)/shard_map/all_to_all | solution.py:33
  84.6 9.3 %all-to-all-start.2 = ((s32[64,1,1]{2,1,0:T(1,128)}), s32[64,1,1]{2,1,0:T(1,128)S(1)}, u32[]{:S(2)}, u32[]{:S(2)}) async-start(s32[64,1,1]{2,1,0:T(1,128)} %copy.24), calls=%async_computation.2 | async-start | bytes 65536 | tf_op jit(solution)/shard_map/all_to_all | solution.py:71
  93.9 8.4 %fusion.13 = f32[128,64,128]{2,1,0:T(8,128)S(1)} fusion(f32[128,64,128]{2,0,1:T(8,128)} %all-to-all-done), kind=kOutput, calls=%fused_computation.19 | convolution fusion | flops 805396480 | bytes 8388608 | tf_op jit(solution)/shard_map/gwf,aw->gaf/dot_general | solution.py:34
  102.3 4.4 copy.27
  106.7 9.2 %all-to-all-start.1 = ((f32[128,64,128]{2,0,1:T(8,128)}), f32[128,64,128]{2,0,1:T(8,128)}, u32[]{:S(2)}, u32[]{:S(2)}) async-start(f32[128,64,128]{2,0,1:T(8,128)} %copy.27), calls=%async_computation.1 | async-start | bytes 8388608 | tf_op jit(solution)/shard_map/all_to_all | solution.py:40
  117.2 49.8 %all-to-all-done.1 = f32[128,64,128]{2,0,1:T(8,128)} async-done(((f32[128,64,128]{2,0,1:T(8,128)}), f32[128,64,128]{2,0,1:T(8,128)}, u32[]{:S(2)}, u32[]{:S(2)}) %all-to-all-start.1) | async-done | bytes 4194336 | tf_op jit(solution)/shard_map/all_to_all | solution.py:40
  167.1 4.9 broadcast_multiply_fusion
  172.0 4.9 gather_fusion.1
  176.9 4.5 select_bitcast_fusion
  181.3 9.4 %all-to-all-start.3 = ((f32[128,64,128]{2,0,1:T(8,128)}), f32[128,64,128]{2,0,1:T(8,128)}, u32[]{:S(2)}, u32[]{:S(2)}) async-start(f32[128,64,128]{2,0,1:T(8,128)} %select_bitcast_fusion), calls=%async_computation.3 | async-start | bytes 8388608 | tf_op jit(solution)/shard_map/all_to_all | solution.py:74
  192.8 49.0 %all-to-all-done.3 = f32[128,64,128]{2,0,1:T(8,128)} async-done(((f32[128,64,128]{2,0,1:T(8,128)}), f32[128,64,128]{2,0,1:T(8,128)}, u32[]{:S(2)}, u32[]{:S(2)}) %all-to-all-start.3) | async-done | bytes 4194336 | tf_op jit(solution)/shard_map/all_to_all | solution.py:74
  241.8 4.9 gather_fusion.2
  246.7 6.5 %multiply_bitcast_fusion = f32[128,64,128]{2,0,1:T(8,128)S(1)} fusion(bf16[64,128,128]{2,1,0:T(8,128)(2,1)S(1)} %copy-done, f32[64,128,128]{2,1,0:T(8,128)} %gather_fusion.2, f32[64,128]{1,0:T(8,128)S(1)} %bitcast.57, pred[64]{0:T(512)(128)(4,1)S(1)} %compare_and_fusion), kind=kOutput, calls=%fused_computation.16 | convolution fusion | flops 1612709888 | bytes 10518592 | tf_op jit(solution)/shard_map/rbj,bij->rbi/dot_general | solution.py:76
  253.3 6.5 %fusion.6 = f32[128,64,128]{2,1,0:T(8,128)S(1)} fusion(f32[128,64,128]{2,0,1:T(8,128)S(1)} %multiply_bitcast_fusion), kind=kOutput, calls=%fused_computation.10 | convolution fusion | flops 1611022336 | bytes 8388608 | tf_op jit(solution)/shard_map/rac,dc->rad/dot_general | solution.py:25
  259.8 3.9 convolution_bitcast_fusion
  263.7 2.8 copy.29
  266.5 60.0 %all_to_all.31 = f32[128,64,128]{2,0,1:T(8,128)S(1)} all-to-all(f32[128,64,128]{2,0,1:T(8,128)S(1)} %copy.29), channel_id=1, replica_groups=mesh['feat'=64,'rows'=2] {'feat'}, dimensions={1} | all-to-all | bytes 8388608 | tf_op jit(solution)/shard_map/all_to_all | solution.py:33
  326.5 6.0 %fusion.16 = f32[128,64,128]{2,1,0:T(8,128)S(1)} fusion(f32[128,64,128]{2,0,1:T(8,128)S(1)} %all_to_all.31), kind=kOutput, calls=%fused_computation.20 | convolution fusion | flops 805396480 | bytes 8388608 | tf_op jit(solution)/shard_map/gwf,aw->gaf/dot_general | solution.py:34
  332.5 4.4 copy.31
  336.9 6.1 %all-to-all-start.5 = ((f32[128,64,128]{2,0,1:T(8,128)}), f32[128,64,128]{2,0,1:T(8,128)}, u32[]{:S(2)}, u32[]{:S(2)}) async-start(f32[128,64,128]{2,0,1:T(8,128)} %copy.31), calls=%async_computation.5 | async-start | bytes 8388608 | tf_op jit(solution)/shard_map/all_to_all | solution.py:40
  344.3 49.6 %all-to-all-done.5 = f32[128,64,128]{2,0,1:T(8,128)} async-done(((f32[128,64,128]{2,0,1:T(8,128)}), f32[128,64,128]{2,0,1:T(8,128)}, u32[]{:S(2)}, u32[]{:S(2)}) %all-to-all-start.5) | async-done | bytes 4194336 | tf_op jit(solution)/shard_map/all_to_all | solution.py:40
  393.9 5.6 copy.32
  399.5 16.6 %fusion.1 = f32[128,8192]{0,1:T(8,128)S(1)} fusion(f32[128,64,128]{0,2,1:T(8,128)} %copy.32, f32[8192]{0:T(1024)S(1)} %copy-done.5, f32[8192]{0:T(1024)S(1)} %broadcast_multiply_fusion.2), kind=kLoop, calls=%fused_computation.5 | loop fusion | flops 2097152 | bytes 8454144 | tf_op jit(solution)/shard_map/cos | solution.py:84
  420.6 142.3 %psum.7 = f32[128]{0:T(128)S(1)} all-reduce(f32[128]{0:T(128)S(1)} %convolution_bitcast_fusion.2), channel_id=1, replica_groups=mesh['feat'=64,'rows'=2] {'feat'}, use_global_device_ids=true, to_apply=%region_2.4 | all-reduce | flops 128 | bytes 1024 | tf_op jit(solution)/shard_map/psum | solution.py:86
  562.9 5.6 fusion.36
  568.6 11.9 %all-reduce = f32[8192]{0:T(1024)S(1)} all-reduce(f32[8192]{0:T(1024)S(1)} %broadcast_multiply_fusion.1), channel_id=2, replica_groups=mesh['feat'=64,'rows'=2] {'rows'}, use_global_device_ids=true, to_apply=%region_3.5.clone | all-reduce | flops 8192 | bytes 65536
  (48 shorter events, 12.6 us)
Async XLA Ops:
  0.6 246.1 %copy-start = (bf16[64,128,128]{2,1,0:T(8,128)(2,1)S(1)}, bf16[64,128,128]{2,1,0:T(8,128)(2,1)}, u32[]{:S(2)}) copy-start(bf16[64,128,128]{2,1,0:T(8,128)(2,1)} %param.17) | copy-start | bytes 6291460
  4.2 4.8 copy-start.3
  23.7 9.8 %copy-start.10 = (s32[64]{0:T(128)S(1)}, s32[64]{0:T(128)}, u32[]{:S(2)}) copy-start(s32[64]{0:T(128)} %param.16) | copy-start | bytes 772
  23.7 60.9 %all-to-all-start = ((f32[128,64,128]{2,0,1:T(8,128)}), f32[128,64,128]{2,0,1:T(8,128)}, u32[]{:S(2)}, u32[]{:S(2)}) async-start(f32[128,64,128]{2,0,1:T(8,128)} %copy.25), calls=%async_computation | async-start | bytes 8388608 | tf_op jit(solution)/shard_map/all_to_all | solution.py:33
  84.6 22.1 %all-to-all-start.2 = ((s32[64,1,1]{2,1,0:T(1,128)}), s32[64,1,1]{2,1,0:T(1,128)S(1)}, u32[]{:S(2)}, u32[]{:S(2)}) async-start(s32[64,1,1]{2,1,0:T(1,128)} %copy.24), calls=%async_computation.2 | async-start | bytes 65536 | tf_op jit(solution)/shard_map/all_to_all | solution.py:71
  106.7 60.3 %all-to-all-start.1 = ((f32[128,64,128]{2,0,1:T(8,128)}), f32[128,64,128]{2,0,1:T(8,128)}, u32[]{:S(2)}, u32[]{:S(2)}) async-start(f32[128,64,128]{2,0,1:T(8,128)} %copy.27), calls=%async_computation.1 | async-start | bytes 8388608 | tf_op jit(solution)/shard_map/all_to_all | solution.py:40
  181.3 60.5 %all-to-all-start.3 = ((f32[128,64,128]{2,0,1:T(8,128)}), f32[128,64,128]{2,0,1:T(8,128)}, u32[]{:S(2)}, u32[]{:S(2)}) async-start(f32[128,64,128]{2,0,1:T(8,128)} %select_bitcast_fusion), calls=%async_computation.3 | async-start | bytes 8388608 | tf_op jit(solution)/shard_map/all_to_all | solution.py:74
  192.8 54.0 %copy-start.4 = (f32[8192]{0:T(1024)S(1)}, f32[8192]{0:T(1024)}, u32[]{:S(2)}) copy-start(f32[8192]{0:T(1024)} %param.13) | copy-start | bytes 98308
  336.9 6.1 %copy-start.11 = (u32[128]{0:T(128)S(1)}, u32[128]{0:T(128)}, u32[]{:S(2)}) copy-start(u32[128]{0:T(128)} %constant.76) | copy-start | bytes 1540
  336.9 7.4 %copy-start.7 = (f32[8192]{0:T(1024)S(1)}, f32[8192]{0:T(1024)}, u32[]{:S(2)}) copy-start(f32[8192]{0:T(1024)} %param.14) | copy-start | bytes 98308
  336.9 57.0 %all-to-all-start.5 = ((f32[128,64,128]{2,0,1:T(8,128)}), f32[128,64,128]{2,0,1:T(8,128)}, u32[]{:S(2)}, u32[]{:S(2)}) async-start(f32[128,64,128]{2,0,1:T(8,128)} %copy.31), calls=%async_computation.5 | async-start | bytes 8388608 | tf_op jit(solution)/shard_map/all_to_all | solution.py:40
  344.3 55.2 %copy-start.5 = (f32[8192]{0:T(1024)S(1)}, f32[8192]{0:T(1024)}, u32[]{:S(2)}) copy-start(f32[8192]{0:T(1024)} %param.15) | copy-start | bytes 98308
  399.5 18.8 %copy-start.6 = (f32[8192]{0:T(1024)S(1)}, f32[8192]{0:T(1024)}, u32[]{:S(2)}) copy-start(f32[8192]{0:T(1024)} %param.18) | copy-start | bytes 98308
  416.1 2.1 copy-start.2
  416.1 146.8 %copy-start.8 = (f32[128]{0:T(128)S(1)}, f32[128]{0:T(128)}, u32[]{:S(2)}) copy-start(f32[128]{0:T(128)} %param.19) | copy-start | bytes 1540
  416.1 165.0 %copy-start.1 = (bf16[64,128,128]{2,1,0:T(8,128)(2,1)S(1)}, bf16[64,128,128]{2,1,0:T(8,128)(2,1)}, u32[]{:S(2)}) copy-start(bf16[64,128,128]{2,1,0:T(8,128)(2,1)} %param.17) | copy-start | bytes 6291460
  562.9 18.2 %copy-start.9 = (f32[128]{0:T(128)}, f32[128]{0:T(128)S(1)}, u32[]{:S(2)}) copy-start(f32[128]{0:T(128)S(1)} %broadcast_multiply_fusion.3) | copy-start | bytes 1540
where the time goes:
time: 591 us; the launch traced here: 581 us
  blocking collectives  214 us (36%)
  waiting for transfers between devices  196 us (33%)
  matrix products  49.6 us (8%)
  local copies, waits for them, and re-layouts  44.6 us (8%)
  starting transfers between devices  43.8 us (7%)
  other arithmetic  31.4 us (5%)
    psum x1, blocking collectives, local(): predictions = lax.psum(local_sum, 'feat') * (1.0 / math.sqrt(FEATURE_COUNT))  142 us
    all_to_all x2, waiting for transfers between devices, transform(): lax.all_to_all(combined, 'feat', split_axis=1, concat_axis=1, tiled=True)  99.5 us
    all_to_all x1, blocking collectives, transform(): lax.all_to_all(spread, 'feat', split_axis=1, concat_axis=1, tiled=True)  60 us
    all_to_all x1, waiting for transfers between devices, local(): lax.all_to_all(outgoing, 'feat', split_axis=1, concat_axis=1, tiled=True)  49 us
    all_to_all x1, waiting for transfers between devices, transform(): lax.all_to_all(spread, 'feat', split_axis=1, concat_axis=1, tiled=True)  47.5 us
    cos x1, other arithmetic, local(): features = jnp.cos(scales[None, :] * second + phases[None, :])  16.6 us
    all_to_all x2, starting transfers between devices, transform(): lax.all_to_all(combined, 'feat', split_axis=1, concat_axis=1, tiled=True)  15.3 us
    dot_general x2, matrix products, transform(): jnp.einsum('gwf,aw->gaf', across_devices, rademacher_signs(device_shards)...  14.4 us
  transfers between devices with their start and end apart: 5, of which 4 were waited for; matrix products, arithmetic and copies ran while one was open for 3% of the time, Pallas kernels for 0%

commit v1 on v0

v1 whole, which is shorter than its diff:
```python
import functools
import math

import jax
import jax.numpy as jnp
from jax import lax
from jax.experimental import pallas as pl
from jax.experimental.pallas import tpu as pltpu
from jax.sharding import PartitionSpec as P

FEATURE_COUNT = 524288
LANES = 128
N_BLOCKS = 4096
F32 = jnp.float32
BF16 = jnp.bfloat16


def signs_128():
    i = lax.broadcasted_iota(jnp.int32, (LANES, LANES), 0)
    j = lax.broadcasted_iota(jnp.int32, (LANES, LANES), 1)
    v = jnp.bitwise_and(i, j)
    v = jnp.bitwise_xor(v, jnp.right_shift(v, 4))
    v = jnp.bitwise_xor(v, jnp.right_shift(v, 2))
    v = jnp.bitwise_xor(v, jnp.right_shift(v, 1))
    return (1 - 2 * jnp.bitwise_and(v, 1)).astype(F32).astype(BF16)


def pieces(x):
    a = x.astype(BF16)
    rest = x - a.astype(F32)
    b = rest.astype(BF16)
    c = (rest - b.astype(F32)).astype(BF16)
    return a, b, c


def times_h(x, h2, h1):
    a, b, c = pieces(x)
    ab = jnp.concatenate([a, b], axis=1)
    return jnp.dot(ab, h2, preferred_element_type=F32) + jnp.dot(
        c, h1, preferred_element_type=F32
    )


def h_times(x, h2, h1):
    a, b, c = pieces(x)
    ab = jnp.concatenate([a, b], axis=0)
    return jnp.dot(h2, ab, preferred_element_type=F32) + jnp.dot(
        h1, c, preferred_element_type=F32
    )


def butterfly(values):
    n = len(values)
    half = 1
    values = list(values)
    while half < n:
        out = [None] * n
        for base in range(0, n, 2 * half):
            for k in range(half):
                u, v = values[base + k], values[base + half + k]
                out[base + k] = u + v
                out[base + half + k] = u - v
        values = out
        half *= 2
    return values


TWO_PI_A = 6.28125
TWO_PI_B = 2.0 * math.pi - 6.28125


def cos_coefficients():
    import numpy as np

    n = 7
    k = np.arange(n)
    u = 0.5 * math.pi**2 * (1.0 + np.cos((k + 0.5) * math.pi / n)) * 1.01
    v = np.stack([u**p for p in range(n)], axis=1)
    c = np.linalg.solve(v, np.cos(np.sqrt(u)))
    return [float(x) for x in c]


COS = cos_coefficients()


def cosine(x):
    n = jnp.round(x * (1.0 / (2.0 * math.pi)))
    r = (x - n * TWO_PI_A) - n * TWO_PI_B
    u = r * r
    acc = COS[-1] * u + COS[-2]
    for c in COS[-3::-1]:
        acc = acc * u + c
    return acc


def head_kernel(
    places_ref, targets_ref, emb_ref, gathered_ref, grad_ref, pred_ref,
    emb32, part, first, placed, feats,
):
    me = lax.axis_index("feat")
    h1 = signs_128()
    h2r = jnp.concatenate([h1, h1], axis=0)
    h2l = jnp.concatenate([h1, h1], axis=1)
    for d in range(4):
        emb32[d] = emb_ref[:, d * LANES : (d + 1) * LANES].astype(F32)
    emb = [
        [emb32[d, pl.ds(2 * me + r, 1), :] for d in range(4)]
        for r in range(2)
    ]

    for k_hi in range(8):
        for d in range(4):
            s = gathered_ref[0, pl.ds(512 * k_hi + d, LANES, stride=4), :]
            part[k_hi, d] = jnp.dot(h1, s.astype(BF16), preferred_element_type=F32)

    def stage_u(t, _):
        rows = pl.ds(pl.multiple_of(8 * t, 8), 8)
        cols = []
        for d in range(4):
            cols.append(butterfly([part[k, d, rows, :] for k in range(8)]))
        for k in range(8):
            for r in range(2):
                u = butterfly([emb[r][d] * cols[d][k] for d in range(4)])
                for c in range(4):
                    placed[r, pl.ds(pl.multiple_of(1024 * c + 128 * k + 8 * t, 8), 8), :] = u[c]
        return 0

    lax.fori_loop(0, 16, stage_u, 0)

    for r in range(2):

        def stage_f(t, _, r=r):
            rows = pl.ds(pl.multiple_of(256 * t, 256), 256)
            first[r, rows, :] = times_h(placed[r, rows, :], h2r, h1)
            return 0

        lax.fori_loop(0, 16, stage_f, 0)

    def stage_g(t, _):
        for q in range(16):
            b = 16 * t + q
            s = places_ref[b]
            for r in range(2):
                placed[r, pl.ds(b, 1), :] = first[r, pl.ds(s, 1), :]
        return 0

    lax.fori_loop(0, N_BLOCKS // 16, stage_g, 0)

    def stage_m(t, _):
        xs = [[], []]
        for q in range(16):
            rows = pl.ds(pl.multiple_of(128 * t + 8 * q, 8), 8)
            order = gathered_ref[1, rows, :].astype(jnp.int32)
            g = gathered_ref[2, rows, :]
            for r in range(2):
                x = placed[r, rows, :]
                xs[r].append(jnp.take_along_axis(x, order, axis=1) * g)
        rows = pl.ds(pl.multiple_of(128 * t, 128), 128)
        for r in range(2):
            x = jnp.concatenate(xs[r], axis=0)
            first[r, rows, :] = h_times(times_h(x, h2r, h1), h2l, h1)
        return 0

    lax.fori_loop(0, 32, stage_m, 0)

    def stage_c(t, acc):
        out = []
        for r in range(2):
            row = [pl.ds(pl.multiple_of(128 * k + 8 * t, 8), 8) for k in range(32)]
            y = butterfly([first[r, row[k], :] for k in range(32)])
            total = acc[r]
            for k in range(32):
                scale = gathered_ref[3, row[k], :] * (1.0 / FEATURE_COUNT)
                f = cosine(scale * y[k] + gathered_ref[4, row[k], :])
                feats[r, row[k], :] = f
                total = total + f * gathered_ref[5, row[k], :]
            out.append(total)
        return tuple(out)

    zero = jnp.zeros((8, LANES), F32)
    acc = lax.fori_loop(0, 16, stage_c, (zero, zero))
    residual = []
    for r in range(2):
        p = jnp.sum(acc[r], axis=(0, 1), keepdims=True) * (1.0 / math.sqrt(FEATURE_COUNT))
        pred_ref[r] = jnp.broadcast_to(p, (8, LANES))
        residual.append((p - targets_ref[2 * me + r]) * (1.0 / 16.0))

    def stage_r(t, _):
        rows = pl.ds(pl.multiple_of(64 * t, 64), 64)
        grad_ref[rows, :] = feats[0, rows, :] * residual[0] + feats[1, rows, :] * residual[1]
        return 0

    lax.fori_loop(0, 64, stage_r, 0)


def local(
    embeddings,
    sign_flips,
    gaussian,
    scales,
    phases,
    source_blocks,
    block_permutations,
    weights,
    targets,
):
    order = jnp.einsum(
        "bij,j->bi", block_permutations, jnp.arange(LANES, dtype=BF16),
        preferred_element_type=F32,
    )
    rows = lambda v: v.reshape(-1, LANES)
    packed = jnp.stack(
        [rows(sign_flips), order, rows(gaussian), rows(scales), rows(phases), rows(weights)]
    )
    gathered = lax.all_gather(packed, "feat", axis=1, tiled=True)
    places = lax.all_gather((source_blocks % 4) * 1024 + source_blocks // 4, "feat", tiled=True)
    vmem = pl.BlockSpec(memory_space=pltpu.VMEM)
    smem = pl.BlockSpec(memory_space=pltpu.SMEM)
    field = pltpu.VMEM((2, N_BLOCKS, LANES), F32)
    grads, preds = pl.pallas_call(
        head_kernel,
        out_shape=(
            jax.ShapeDtypeStruct((N_BLOCKS, LANES), F32),
            jax.ShapeDtypeStruct((2, 8, LANES), F32),
        ),
        in_specs=[smem, smem, vmem, vmem],
        out_specs=(vmem, vmem),
        scratch_shapes=[
            pltpu.VMEM((4, 128, LANES), F32),
            pltpu.VMEM((8, 4, LANES, LANES), F32),
            field, field, field,
        ],
        compiler_params=pltpu.CompilerParams(vmem_limit_bytes=60 * 2**20),
    )(places, targets, embeddings, gathered)
    predictions = lax.all_gather(preds[:, 0, 0], "feat", tiled=True)
    feature_grad = lax.psum_scatter(
        grads.reshape(-1), ("feat", "rows"), scatter_dimension=0, tiled=True
    )
    return predictions, feature_grad


def solution(mesh):
    in_specs = (
        P("rows", None), P("feat"), P("feat"), P("feat"), P("feat"), P("feat"),
        P("feat", None, None), P("feat"), P("rows"),
    )
    out_specs = (P("rows"), P(("feat", "rows")))
    return jax.shard_map(local, mesh=mesh, in_specs=in_specs, out_specs=out_specs, check_vma=False)
```

time: 591 us -> 491 us (0.83)
  the two profiles are of different devices: /device:TPU:0 before, /device:TPU:1 now
where the time goes in v1:
time: 491 us
  blocking collectives  422 us (86%)
  Pallas kernels  40.4 us (8%)
  between operations  15.5 us (3%)
  waiting for transfers between devices  7.44 us (2%)
  local copies, waits for them, and re-layouts  5.2 us (1%)
    unnamed x1, blocking collectives  277 us
    all_gather x1, blocking collectives, local(): predictions = lax.all_gather(preds[:, 0, 0], 'feat', tiled=True)  145 us
    pallas_call x1, Pallas kernels, local(): pl.pallas_call(head_kernel, out_shape=(jax.ShapeDtypeStruct((N_BLOCKS, LA...  40.4 us
  transfers between devices with their start and end apart: 2, of which 1 were waited for; matrix products, arithmetic and copies ran while one was open for 0% of the time, Pallas kernels for 0%

profile of v1, /device:TPU:1, one launch (start us, length us, event | category | flops | bytes accessed | tf_op | source)
XLA Modules:
  0.0 491.0 jit_solution(2389275575378488866)
XLA Ops:
  7.2 0.0 copy-start
  7.2 0.0 copy-start.7
  7.2 0.0 copy-start.2
  7.2 0.0 copy-start.3
  7.2 0.0 copy-start.4
  7.2 0.0 copy-start.5
  7.2 0.0 copy-start.6
  7.2 0.0 all-gather.3.cloned.1.call-start
  7.3 0.9 bitcast_dynamic-update-slice_fusion.4
  8.2 0.7 copy-done
  8.8 0.6 fusion.3
  9.5 0.0 copy-done.2
  9.5 0.0 copy-done.3
  9.5 0.0 copy-done.4
  9.6 0.0 copy-done.5
  9.6 0.0 copy-start.1
  9.6 0.7 copy-done.1
  10.3 0.0 all-gather.3.cloned.1.call-update
  10.3 0.0 all-reduce.5.cloned.1.call-start
  10.3 0.0 copy-done.7
  10.3 0.6 dynamic-slice
  11.6 0.0 copy-done.6
  11.6 0.1 fusion.2
  11.7 276.6 %all-reduce.places_ref = s32[4096]{0:T(1024)} all-reduce(s32[4096]{0:T(1024)S(1)} %fusion.2), channel_id=1, replica_groups=mesh['feat'=64,'rows'=2] {'feat'}, use_global_device_ids=true, to_apply=%add | all-reduce | flops 4096 | bytes 32768
  288.3 0.0 all-gather.3.cloned.1.call-done.gathered_ref
  288.3 40.4 %shard_map.104 = (f32[4096,128]{1,0:T(8,128)}, f32[2,8,128]{2,1,0:T(8,128)}) custom-call(s32[4096]{0:T(1024)} %all-reduce.places_ref, f32[128]{0:T(128)} %targets_ref.1, bf16[128,512]{1,0:T(8,128)(2,1)} %emb_ref.1, f32[6,4096,128]{2,1,0:T(8,128)} %all-gather.3.cloned.1.call-done.gathered_ref), custom_call_target="tpu_custom_call" | custom-call | tf_op jit(solution)/shard_map/pallas_call | solution.py:220
  328.7 0.0 all-reduce.5.cloned.1.call-update
  329.4 0.8 slice_reduce_fusion
  330.2 0.2 dynamic-update-slice.1
  330.4 145.0 %all-reduce.1 = f32[128]{0:T(128)} all-reduce(f32[128]{0:T(128)S(1)} %dynamic-update-slice.1), channel_id=2, replica_groups=mesh['feat'=64,'rows'=2] {'feat'}, use_global_device_ids=true, to_apply=%add.1 | all-reduce | flops 128 | bytes 1024 | tf_op jit(solution)/shard_map/all_gather | solution.py:235
  475.4 7.4 %all-reduce.5.cloned.1.call-done = f32[524288]{0:T(1024)} async-done(((f32[524288]{0:T(1024)}), f32[524288]{0:T(1024)}) %all-reduce.5.cloned.1.call-update) | async-done | bytes 2097168
  482.8 1.3 dynamic-slice.2
  (7 shorter events, 0.0 us)
Async XLA Ops:
  7.2 1.7 copy-start
  7.2 3.2 copy-start.7
  7.2 2.3 copy-start.2
  7.2 2.3 copy-start.3
  7.2 2.3 copy-start.4
  7.2 2.3 copy-start.5
  7.2 4.4 copy-start.6
  7.2 281.1 %all-gather.3.cloned.1.call-start = ((), (), s32[]{:S(2)}) async-start(), calls=%async_computation | async-start | bytes 12779520 | tf_op jit(solution)/shard_map/all_gather | solution.py:215
  9.6 0.7 copy-start.1
  10.3 472.6 %all-reduce.5.cloned.1.call-start = ((), (), s32[]{:S(2)}) async-start(), calls=%async_computation.1 | async-start | bytes 4194304
Sparse Core Ops, SparseCore 0:
  10.4 119.7 all-gather.2
  328.9 153.9 all-reduce.4

commit v2 on v1

--- a/solution.py
+++ b/solution.py
@@ -93,6 +93,324 @@
     return acc
 
 
+MESH = pl.DeviceIdType.MESH
+ALL = slice(None)
+ORDERS = ("zyx", "zxy", "yxz", "xyz")
+STREAM_SEMS = 16
+
+
+class Place:
+    def __init__(self):
+        me = lax.axis_index("feat")
+        self.h = lax.axis_index("rows")
+        self.c = lax.rem(me, 2)
+        self.z = lax.rem(me // 2, 2)
+        self.y = lax.rem(me // 4, 4)
+        self.x = me // 16
+        self.zz = 2 * self.h + self.z
+
+    def at(self, x=None, y=None, z=None, c=None, h=None):
+        x = self.x if x is None else x
+        y = self.y if y is None else y
+        z = self.z if z is None else z
+        c = self.c if c is None else c
+        h = self.h if h is None else h
+        return (((x * 4 + y) * 2 + z) * 2 + c, h)
+
+    def along(self, dim, step):
+        a = lax.rem(getattr(self, dim) + 4 + step, 4)
+        if dim == "zz":
+            return self.at(z=lax.rem(a, 2), h=a // 2)
+        return self.at(**{dim: a})
+
+    def neighbours(self):
+        out = [self.along(d, s) for d in ("x", "y", "zz") for s in (1, -1)]
+        return out + [self.at(c=1 - self.c), self.along("zz", 2)]
+
+
+def greet(place):
+    barrier = pltpu.get_barrier_semaphore()
+    others = place.neighbours()
+    for device in others:
+        pl.semaphore_signal(barrier, inc=1, device_id=device, device_id_type=MESH)
+    pl.semaphore_wait(barrier, len(others))
+
+
+class Sender:
+    def __init__(self, send, recv):
+        self.send, self.recv = send, recv
+        self.started = []
+
+    def copy(self, ref, dst, sem, device):
+        return pltpu.make_async_remote_copy(
+            src_ref=ref, dst_ref=dst, send_sem=self.send.at[sem], recv_sem=self.recv.at[sem],
+            device_id=device, device_id_type=MESH,
+        )
+
+    def start(self, ref, dst, sem, device):
+        copy = self.copy(ref, dst, sem, device)
+        copy.start()
+        self.started.append(copy)
+
+    def arrived(self, ref, sem, device):
+        self.copy(ref, ref, sem, device).wait_recv()
+
+    def finish(self):
+        for copy in self.started:
+            copy.wait_send()
+
+
+def gather_stream(place, sender, base, order, get, halves):
+    sel = {"x": place.x, "y": place.y, "z": place.z, "c": place.c}
+    partner = place.at(c=1 - place.c)
+    sem = base
+    mirrored = []
+
+    def mirror(index, **where):
+        here = get({**sel, **where}, None)
+        sender.start(here, here, index, partner)
+        mirrored.append((get({**sel, **where, "c": 1 - place.c}, None), index))
+
+    last = len(order) - 1
+    for phase, dim in enumerate(order):
+        final = phase == last
+        if dim == "z":
+            other = 1 - place.z
+            ways = ((0, place.h), (1, 1 - place.h)) if halves else ((None, place.h),)
+            for k, (half, h) in enumerate(ways):
+                ref = get(sel, half)
+                sender.start(ref, ref, sem + k, place.at(z=other, h=h))
+            if final:
+                mirror(base + 12)
+            yield
+            for k, (half, h) in enumerate(ways):
+                sender.arrived(get({**sel, "z": other}, half), sem + k, place.at(z=other, h=h))
+            if final:
+                mirror(base + 13, z=other)
+            sem += 2
+        else:
+            a = sel[dim]
+            up, down = place.along(dim, 1), place.along(dim, -1)
+            above, below = lax.rem(a + 1, 4), lax.rem(a + 3, 4)
+            across = lax.rem(a + 2, 4)
+            own = get(sel, None)
+            sender.start(own, own, sem, up)
+            sender.start(own, own, sem + 1, down)
+            if final:
+                mirror(base + 12)
+            yield
+            sender.arrived(get({**sel, dim: below}, None), sem, down)
+            ref = get({**sel, dim: below}, 0 if halves else None)
+            sender.start(ref, ref, sem + 2, up)
+            sender.arrived(get({**sel, dim: above}, None), sem + 1, up)
+            if halves:
+                ref = get({**sel, dim: above}, 1)
+                sender.start(ref, ref, sem + 3, down)
+            if final:
+                mirror(base + 13, **{dim: below})
+                mirror(base + 14, **{dim: above})
+            yield
+            sender.arrived(get({**sel, dim: across}, 0 if halves else None), sem + 2, down)
+            if halves:
+                sender.arrived(get({**sel, dim: across}, 1), sem + 3, up)
+            if final:
+                mirror(base + 15, **{dim: across})
+            sem += 4
+        sel[dim] = ALL
+    yield
+    for ref, index in mirrored:
+        sender.arrived(ref, index, partner)
+
+
+def run_streams(streams):
+    live = list(streams)
+    while live:
+        left = []
+        for s in live:
+            try:
+                next(s)
+                left.append(s)
+            except StopIteration:
+                pass
+        live = left
+
+
+GROUPS = ((0, 1), (1, 3), (3, 6))
+
+
+def gather_kernel(
+    sources_ref, signs_ref, gaussian_ref, scales_ref, phases_ref, weights_ref, perms_ref,
+    out_ref, places_ref,
+    perms, send, recv, own,
+):
+    place = Place()
+    x, y, z, c = place.x, place.y, place.z, place.c
+    given = [signs_ref, None, gaussian_ref, scales_ref, phases_ref, weights_ref]
+    copies = [pltpu.make_async_copy(perms_ref, perms, own.at[6])]
+    for v, ref in enumerate(given):
+        if ref is not None:
+            copies.append(pltpu.make_async_copy(ref, out_ref.at[v, x, y, z, c], own.at[v]))
+    copies.append(pltpu.make_async_copy(sources_ref, places_ref.at[x, y, z, c], own.at[7]))
+    for copy in copies:
+        copy.start()
+    greet(place)
+    for copy in copies:
+        copy.wait()
+    sender = Sender(send, recv)
+
+    def getter(group, part):
+        vs = slice(*GROUPS[group])
+
+        def get(sel, half):
+            rows = pl.ds(16 * part, 16) if half is None else pl.ds(16 * part + 8 * half, 8)
+            return out_ref.at[vs, sel["x"], sel["y"], sel["z"], sel["c"], rows, :]
+
+        return get
+
+    def get_places(sel, half):
+        return places_ref.at[sel["x"], sel["y"], sel["z"], sel["c"]]
+
+    streams = []
+    for group in range(3):
+        for part in range(4):
+            base = STREAM_SEMS * (4 * group + part)
+            streams.append(
+                gather_stream(place, sender, base, ORDERS[part], getter(group, part), True)
+            )
+    streams.append(gather_stream(place, sender, STREAM_SEMS * 12, "zyx", get_places, False))
+    for s in streams[:4]:
+        next(s)
+    lanes = lax.broadcasted_iota(jnp.int32, (8, LANES), 1).astype(F32).astype(BF16)
+
+    def order_of(t, _):
+        rows = []
+        for q in range(8):
+            line = lax.dot_general(
+                lanes, perms[8 * t + q], (((1,), (1,)), ((), ())), preferred_element_type=F32
+            )
+            rows.append(line[0:1])
+        out_ref[1, x, y, z, c, pl.ds(pl.multiple_of(8 * t, 8), 8), :] = jnp.concatenate(rows, axis=0)
+        return 0
+
+    lax.fori_loop(0, 8, order_of, 0)
+    for s in streams[4:]:
+        next(s)
+    run_streams(streams)
+    sender.finish()
+
+
+DIMS = ("x", "y", "zz")
+REDUCE_ORDERS = (("x", "y", "zz"), ("y", "zz", "x"), ("zz", "x", "y"), ("zz", "y", "x"))
+
+
+def reduce_scratch():
+    out = []
+    for first, second, _ in REDUCE_ORDERS:
+        wide = [d for d in DIMS if d != first]
+        half = tuple(2 if d == second else 4 for d in wide)
+        for shape in (half, half, (4, 4), (4, 4), (2,), (2,), (4,), (4,)):
+            out.append(pltpu.VMEM(shape + (8, LANES), F32))
+    return out
+
+
+def reduce_part(place, sender, base, p, order, total, slots, last, out_ref):
+    where = {d: None for d in DIMS}
+
+    def cut(dim, index, rest=None, side=None):
+        parts = []
+        for d in DIMS:
+            if d == dim:
+                parts.append(index)
+            elif where[d] is not None:
+                parts.append(where[d])
+            elif d == rest:
+                parts.append(pl.ds(2 * side, 2))
+            else:
+                parts.append(ALL)
+        return (p, *parts)
+
+    for phase, dim in enumerate(order):
+        a = getattr(place, dim)
+        up, down = place.along(dim, 1), place.along(dim, -1)
+        above, below, across = lax.rem(a + 1, 4), lax.rem(a + 3, 4), lax.rem(a + 2, 4)
+        sem = base + 4 * phase
+        if phase < 2:
+            rest = order[phase + 1]
+            half_up, half_down, whole_up, whole_down = slots[4 * phase : 4 * phase + 4]
+            sender.start(total.at[cut(dim, across, rest, 0)], half_up, sem, up)
+            sender.start(total.at[cut(dim, across, rest, 1)], half_down, sem + 1, down)
+            yield
+            sender.arrived(half_up, sem, down)
+            i = cut(dim, above, rest, 0)
+            total[i] = total[i] + half_up[...]
+            sender.start(total.at[cut(dim, above)], whole_up, sem + 2, up)
+            sender.arrived(half_down, sem + 1, up)
+            i = cut(dim, below, rest, 1)
+            total[i] = total[i] + half_down[...]
+            sender.start(total.at[cut(dim, below)], whole_down, sem + 3, down)
+            yield
+            sender.arrived(whole_up, sem + 2, down)
+            sender.arrived(whole_down, sem + 3, up)
+            i = cut(dim, a)
+            total[i] = total[i] + (whole_up[...] + whole_down[...])
+        else:
+            far = place.along(dim, 2)
+            sender.start(total.at[cut(dim, above)], last.at[p, 0], sem, up)
+            sender.start(total.at[cut(dim, below)], last.at[p, 1], sem + 1, down)
+            sender.start(total.at[cut(dim, across)], last.at[p, 2], sem + 2, far)
+            yield
+            sender.arrived(last.at[p, 0], sem, down)
+            sender.arrived(last.at[p, 1], sem + 1, up)
+            sender.arrived(last.at[p, 2], sem + 2, far)
+            out_ref[8 * p : 8 * p + 8, :] = total[cut(dim, a)] + (
+                last[p, 0] + last[p, 1] + last[p, 2]
+            )
+        where[dim] = a
+
+
+def reduce_kernel(
+    grads_ref, preds_ref, out_ref, line_ref, theirs, total, last, lines, send, recv, *slots
+):
+    place = Place()
+    x, y, z, c, h = place.x, place.y, place.z, place.c, place.h
+    partner = place.at(c=1 - c)
+    me = ((x * 4 + y) * 2 + z) * 2 + c
+    lane = lax.broadcasted_iota(jnp.int32, (1, LANES), 1)
+    lines[x, y, z, c] = jnp.where(
+        lane == 2 * me, preds_ref[0, 0:1, :],
+        jnp.where(lane == 2 * me + 1, preds_ref[1, 0:1, :], 0.0),
+    )
+    greet(place)
+    sender = Sender(send, recv)
+    for p in range(4):
+        sender.start(grads_ref.at[:, :, :, 1 - c, :, p], theirs.at[p], 16 * p, partner)
+
+    def get_lines(sel, half):
+        return lines.at[sel["x"], sel["y"], sel["z"], sel["c"]]
+
+    def part(p):
+        sender.arrived(theirs.at[p], 16 * p, partner)
+        for hh in range(2):
+            for zed in range(2):
+                total[p, :, :, 2 * hh + zed] = (
+                    grads_ref[:, :, zed, c, hh, p] + theirs[p, :, :, zed, hh]
+                )
+        yield from reduce_part(
+            place, sender, 16 * p + 1, p, REDUCE_ORDERS[p], total, slots[8 * p : 8 * p + 8],
+            last, out_ref,
+        )
+
+    run_streams(
+        [part(p) for p in range(4)]
+        + [gather_stream(place, sender, 64, "zyx", get_lines, False)]
+    )
+    line = jnp.zeros((1, LANES), F32)
+    for i in range(64):
+        line = line + lines[i // 16, (i // 4) % 4, (i // 2) % 2, i % 2]
+    line_ref[...] = line
+    sender.finish()
+
+
 def head_kernel(
     places_ref, targets_ref, emb_ref, gathered_ref, grad_ref, pred_ref,
     emb32, part, first, placed, feats,
@@ -204,18 +522,35 @@
     weights,
     targets,
 ):
-    order = jnp.einsum(
-        "bij,j->bi", block_permutations, jnp.arange(LANES, dtype=BF16),
-        preferred_element_type=F32,
-    )
     rows = lambda v: v.reshape(-1, LANES)
-    packed = jnp.stack(
-        [rows(sign_flips), order, rows(gaussian), rows(scales), rows(phases), rows(weights)]
-    )
-    gathered = lax.all_gather(packed, "feat", axis=1, tiled=True)
-    places = lax.all_gather((source_blocks % 4) * 1024 + source_blocks // 4, "feat", tiled=True)
     vmem = pl.BlockSpec(memory_space=pltpu.VMEM)
     smem = pl.BlockSpec(memory_space=pltpu.SMEM)
+    any_ = pl.BlockSpec(memory_space=pl.ANY)
+    sources = jnp.pad(source_blocks, (0, 64)).reshape(1, LANES)
+    gathered, sources_all = pl.pallas_call(
+        gather_kernel,
+        out_shape=(
+            jax.ShapeDtypeStruct((6, 4, 4, 2, 2, 64, LANES), F32),
+            jax.ShapeDtypeStruct((4, 4, 2, 2, 1, LANES), jnp.int32),
+        ),
+        in_specs=[vmem] + [any_] * 6,
+        out_specs=(vmem, vmem),
+        scratch_shapes=[
+            pltpu.VMEM((64, LANES, LANES), BF16),
+            pltpu.SemaphoreType.DMA((STREAM_SEMS * 13,)),
+            pltpu.SemaphoreType.DMA((STREAM_SEMS * 13,)),
+            pltpu.SemaphoreType.DMA((8,)),
+        ],
+        compiler_params=pltpu.CompilerParams(
+            vmem_limit_bytes=40 * 2**20, collective_id=0, has_side_effects=True
+        ),
+    )(
+        sources, rows(sign_flips), rows(gaussian), rows(scales), rows(phases), rows(weights),
+        block_permutations,
+    )
+    gathered = gathered.reshape(6, N_BLOCKS, LANES)
+    sources_all = sources_all.reshape(64, LANES)[:, :64].reshape(-1)
+    places = (sources_all % 4) * 1024 + sources_all // 4
     field = pltpu.VMEM((2, N_BLOCKS, LANES), F32)
     grads, preds = pl.pallas_call(
         head_kernel,
@@ -232,11 +567,28 @@
         ],
         compiler_params=pltpu.CompilerParams(vmem_limit_bytes=60 * 2**20),
     )(places, targets, embeddings, gathered)
-    predictions = lax.all_gather(preds[:, 0, 0], "feat", tiled=True)
-    feature_grad = lax.psum_scatter(
-        grads.reshape(-1), ("feat", "rows"), scatter_dimension=0, tiled=True
-    )
-    return predictions, feature_grad
+    grad_out, line = pl.pallas_call(
+        reduce_kernel,
+        out_shape=(
+            jax.ShapeDtypeStruct((32, LANES), F32),
+            jax.ShapeDtypeStruct((1, LANES), F32),
+        ),
+        in_specs=[vmem, vmem],
+        out_specs=(vmem, vmem),
+        scratch_shapes=[
+            pltpu.VMEM((4, 4, 4, 2, 2, 8, LANES), F32),
+            pltpu.VMEM((4, 4, 4, 4, 8, LANES), F32),
+            pltpu.VMEM((4, 3, 8, LANES), F32),
+            pltpu.VMEM((4, 4, 2, 2, 1, LANES), F32),
+            pltpu.SemaphoreType.DMA((80,)),
+            pltpu.SemaphoreType.DMA((80,)),
+            *reduce_scratch(),
+        ],
+        compiler_params=pltpu.CompilerParams(
+            vmem_limit_bytes=40 * 2**20, collective_id=1, has_side_effects=True
+        ),
+    )(grads.reshape(4, 4, 2, 2, 2, 4, 8, LANES), preds)
+    return line.reshape(-1), grad_out.reshape(-1)
 
 
 def solution(mesh):

time: 491 us -> 129 us (0.26)
  blocking collectives: 422 us -> 0 us
  Pallas kernels: 40.4 us -> 118 us
  between operations: 15.5 us -> 0.66 us
  waiting for transfers between devices: 7.44 us -> 0 us
    unnamed x1 -> x0, blocking collectives: 277 us -> none
    all_gather x1 -> x0, blocking collectives: 145 us -> none  [local(): predictions = lax.all_gather(preds[:, 0, 0], 'feat', tiled=True)]
    pallas_call x0 -> x2, Pallas kernels: none -> 77.7 us  [the longest x1 54.5 us: local(): pl.pallas_call(gather_kernel, out_shape=(jax.ShapeDtypeStruct((6, 4, 4, 2...]
    unnamed x3 -> x0, waiting for transfers between devices: 7.44 us -> none
  transfers between devices with their start and end apart: 2 -> 0, of which waited for: 1 -> 0; matrix products, arithmetic and copies ran while one was open for 0% -> 0% of each run, Pallas kernels for 0% -> 0%
where the time goes in v2:
time: 129 us
  Pallas kernels  118 us (91%)
  local copies, waits for them, and re-layouts  9.52 us (7%)
    pallas_call x1, Pallas kernels, local(): pl.pallas_call(gather_kernel, out_shape=(jax.ShapeDtypeStruct((6, 4, 4, 2...  54.5 us
    pallas_call x1, Pallas kernels, local(): pl.pallas_call(head_kernel, out_shape=(jax.ShapeDtypeStruct((N_BLOCKS, LA...  40.4 us
    pallas_call x1, Pallas kernels, local(): pl.pallas_call(reduce_kernel, out_shape=(jax.ShapeDtypeStruct((32, LANES)...  23.2 us
    unnamed x18, local copies, waits for them, and re-layouts  8.78 us

profile of v2, /device:TPU:1, one launch (start us, length us, event | category | flops | bytes accessed | tf_op | source)
XLA Modules:
  0.0 128.9 jit_solution(2358093532057552300)
XLA Ops:
  0.6 0.7 pad_bitcast_fusion.sources_ref
  1.3 0.0 copy-start
  1.3 1.6 %copy-done = bf16[64,128,128]{2,1,0:T(8,128)(2,1)S(1)} copy-done((bf16[64,128,128]{2,1,0:T(8,128)(2,1)S(1)}, bf16[64,128,128]{2,1,0:T(8,128)(2,1)}, u32[]{:S(2)}) %copy-start) | copy-done | bytes 2097176
  2.9 0.0 copy-start.2
  2.9 0.8 copy-done.2
  3.6 0.0 copy-start.3
  3.6 0.8 copy-done.3
  4.4 0.0 copy-start.4
  4.4 0.8 copy-done.4
  5.2 0.0 copy-start.5
  5.2 0.8 copy-done.5
  5.9 0.0 copy-start.6
  5.9 0.8 copy-done.6
  6.7 54.5 %shard_map.104 = (f32[6,4,4,2,2,64,128]{6,5,4,3,2,1,0:T(8,128)}, s32[4,4,2,2,1,128]{5,4,3,2,1,0:T(1,128)S(1)}) custom-call(s32[1,128]{1,0:T(1,128)S(1)} %pad_bitcast_fusion.sources_ref, f32[64,128]{1,0:T(8,128)S(1)} %bitcast.14, f32[64,128]{1,0:T(8,128)S(1)} %bitcast.15, f32[64,128]{1,0:T(8,128)S(1)} %bitcast.16, f32[64,128]{1,0:T(8,128)S(1)} %bitcast.17, ...), custom_call_target="tpu_custom_call" | custom-call | tf_op jit(solution)/shard_map/pallas_call | solution.py:530
  61.2 0.1 reshape.47
  61.2 0.6 fusion.1.places_ref
  61.9 40.4 %shard_map.105 = (f32[4096,128]{1,0:T(8,128)}, f32[2,8,128]{2,1,0:T(8,128)}) custom-call(s32[4096]{0:T(1024)} %fusion.1.places_ref, f32[128]{0:T(128)} %targets_ref.1, bf16[128,512]{1,0:T(8,128)(2,1)} %emb_ref.1, f32[6,4096,128]{2,1,0:T(8,128)} %bitcast.22), custom_call_target="tpu_custom_call" | custom-call | tf_op jit(solution)/shard_map/pallas_call | solution.py:555
  102.2 0.0 copy-start.1
  102.2 1.6 %copy-done.1 = f32[4096,128]{1,0:T(8,128)S(1)} copy-done((f32[4096,128]{1,0:T(8,128)S(1)}, f32[4096,128]{1,0:T(8,128)}, u32[]{:S(2)}) %copy-start.1) | copy-done | bytes 2097176
  103.8 0.0 copy-start.7
  103.8 0.7 copy-done.7
  104.5 23.2 %shard_map.106 = (f32[32,128]{1,0:T(8,128)S(1)}, f32[1,128]{1,0:T(1,128)S(1)}) custom-call(f32[4,4,2,2,2,4,8,128]{7,6,5,4,3,2,1,0:T(8,128)S(1)} %bitcast.13, f32[2,8,128]{2,1,0:T(8,128)S(1)} %copy-done.7), custom_call_target="tpu_custom_call" | custom-call | tf_op jit(solution)/shard_map/pallas_call | solution.py:570
  127.8 0.5 copy.13
  128.3 0.6 copy.14
Async XLA Ops:
  1.3 1.6 %copy-start = (bf16[64,128,128]{2,1,0:T(8,128)(2,1)S(1)}, bf16[64,128,128]{2,1,0:T(8,128)(2,1)}, u32[]{:S(2)}) copy-start(bf16[64,128,128]{2,1,0:T(8,128)(2,1)} %perms_ref.1) | copy-start | bytes 6291460
  2.9 0.8 copy-start.2
  3.6 0.8 copy-start.3
  4.4 0.8 copy-start.4
  5.2 0.8 copy-start.5
  5.9 0.8 copy-start.6
  102.2 1.6 %copy-start.1 = (f32[4096,128]{1,0:T(8,128)S(1)}, f32[4096,128]{1,0:T(8,128)}, u32[]{:S(2)}) copy-start(f32[4096,128]{1,0:T(8,128)} %get-tuple-element.10) | copy-start | bytes 6291460
  103.8 0.7 copy-start.7

commit v3 on v1

v3 whole, which is shorter than its diff:
```python
import functools
import math

import jax
import jax.numpy as jnp
from jax import lax
from jax.experimental import pallas as pl
from jax.experimental.pallas import tpu as pltpu
from jax.sharding import PartitionSpec as P

FEATURE_COUNT = 524288
LANES = 128
N_BLOCKS = 4096
F32 = jnp.float32
BF16 = jnp.bfloat16


def signs_128():
    i = lax.broadcasted_iota(jnp.int32, (LANES, LANES), 0)
    j = lax.broadcasted_iota(jnp.int32, (LANES, LANES), 1)
    v = jnp.bitwise_and(i, j)
    v = jnp.bitwise_xor(v, jnp.right_shift(v, 4))
    v = jnp.bitwise_xor(v, jnp.right_shift(v, 2))
    v = jnp.bitwise_xor(v, jnp.right_shift(v, 1))
    return (1 - 2 * jnp.bitwise_and(v, 1)).astype(F32).astype(BF16)


def times_h(x, h2):
    a = x.astype(BF16)
    b = (x - a.astype(F32)).astype(BF16)
    return jnp.dot(jnp.concatenate([a, b], axis=1), h2, preferred_element_type=F32)


def butterfly(values):
    n = len(values)
    half = 1
    values = list(values)
    while half < n:
        out = [None] * n
        for base in range(0, n, 2 * half):
            for k in range(half):
                u, v = values[base + k], values[base + half + k]
                out[base + k] = u + v
                out[base + half + k] = u - v
        values = out
        half *= 2
    return values


TWO_PI_A = 6.28125
TWO_PI_B = 2.0 * math.pi - 6.28125


def cos_coefficients():
    import numpy as np

    n = 7
    k = np.arange(n)
    u = 0.5 * math.pi**2 * (1.0 + np.cos((k + 0.5) * math.pi / n)) * 1.01
    v = np.stack([u**p for p in range(n)], axis=1)
    c = np.linalg.solve(v, np.cos(np.sqrt(u)))
    return [float(x) for x in c]


COS = cos_coefficients()


def cosine(x):
    n = jnp.round(x * (1.0 / (2.0 * math.pi)))
    r = (x - n * TWO_PI_A) - n * TWO_PI_B
    u = r * r
    acc = COS[-1] * u + COS[-2]
    for c in COS[-3::-1]:
        acc = acc * u + c
    return acc


MESH = pl.DeviceIdType.MESH
ALL = slice(None)
ORDERS = ("zyx", "zxy", "yxz", "xyz")
STREAM_SEMS = 14
DIMS = ("x", "y", "zz")


class Place:
    def __init__(self):
        me = lax.axis_index("feat")
        self.h = lax.axis_index("rows")
        self.c = lax.rem(me, 2)
        self.z = lax.rem(me // 2, 2)
        self.y = lax.rem(me // 4, 4)
        self.x = me // 16
        self.zz = 2 * self.h + self.z

    def at(self, x=None, y=None, z=None, c=None, h=None):
        x = self.x if x is None else x
        y = self.y if y is None else y
        z = self.z if z is None else z
        c = self.c if c is None else c
        h = self.h if h is None else h
        return (((x * 4 + y) * 2 + z) * 2 + c, h)

    def along(self, dim, step):
        a = lax.rem(getattr(self, dim) + 4 + step, 4)
        if dim == "zz":
            return self.at(z=lax.rem(a, 2), h=a // 2)
        return self.at(**{dim: a})

    def neighbours(self):
        out = [self.along(d, s) for d in DIMS for s in (1, -1, 2)]
        return out + [self.at(c=1 - self.c)]


def greet(place):
    barrier = pltpu.get_barrier_semaphore()
    others = place.neighbours()
    for device in others:
        pl.semaphore_signal(barrier, inc=1, device_id=device, device_id_type=MESH)
    pl.semaphore_wait(barrier, len(others))


class Sender:
    def __init__(self, send, recv):
        self.send, self.recv = send, recv
        self.started = []

    def copy(self, ref, dst, sem, device):
        return pltpu.make_async_remote_copy(
            src_ref=ref, dst_ref=dst, send_sem=self.send.at[sem], recv_sem=self.recv.at[sem],
            device_id=device, device_id_type=MESH,
        )

    def start(self, ref, dst, sem, device):
        copy = self.copy(ref, dst, sem, device)
        copy.start()
        self.started.append(copy)

    def arrived(self, ref, sem, device):
        self.copy(ref, ref, sem, device).wait_recv()

    def finish(self):
        for copy in self.started:
            copy.wait_send()


def gather_stream(place, sender, base, order, get, halves):
    sel = {"x": place.x, "y": place.y, "z": place.z, "c": place.c}
    partner = place.at(c=1 - place.c)
    sem = base
    mirrored = []

    def mirror(index, **where):
        here = get({**sel, **where}, None)
        sender.start(here, here, index, partner)
        mirrored.append((get({**sel, **where, "c": 1 - place.c}, None), index))

    for phase, dim in enumerate(order):
        final = phase == 2
        if dim == "z":
            other = 1 - place.z
            ways = ((0, place.h), (1, 1 - place.h)) if halves else ((None, place.h),)
            for k, (half, h) in enumerate(ways):
                ref = get(sel, half)
                sender.start(ref, ref, sem + k, place.at(z=other, h=h))
            if final:
                mirror(base + 10)
            yield
            for k, (half, h) in enumerate(ways):
                sender.arrived(get({**sel, "z": other}, half), sem + k, place.at(z=other, h=h))
            if final:
                mirror(base + 11, z=other)
            sem += 2
        else:
            a = sel[dim]
            own = get(sel, None)
            for k, step in enumerate((1, -1, 2)):
                sender.start(own, own, sem + k, place.along(dim, step))
            if final:
                mirror(base + 10)
            yield
            for k, step in enumerate((-1, 1, 2)):
                there = lax.rem(a + 4 + step, 4)
                sender.arrived(get({**sel, dim: there}, None), sem + k, place.along(dim, step))
                if final:
                    mirror(base + 11 + k, **{dim: there})
            sem += 3
        sel[dim] = ALL
    yield
    for ref, index in mirrored:
        sender.arrived(ref, index, partner)


def run_streams(streams):
    live = list(streams)
    while live:
        left = []
        for s in live:
            try:
                next(s)
                left.append(s)
            except StopIteration:
                pass
        live = left


def advance(streams):
    for s in streams:
        next(s, None)


REDUCE_ORDERS = (("x", "y", "zz"), ("y", "zz", "x"), ("zz", "x", "y"), ("zz", "y", "x"))


def reduce_part(place, sender, base, p, order, total, wide, narrow, last, out_ref):
    where = {d: None for d in DIMS}

    def cut(dim, index):
        parts = []
        for d in DIMS:
            if d == dim:
                parts.append(index)
            else:
                parts.append(ALL if where[d] is None else where[d])
        return (p, *parts)

    for phase, dim in enumerate(order):
        a = getattr(place, dim)
        slots = (wide, narrow, last)[phase]
        sem = base + 3 * phase
        for k, step in enumerate((1, -1, 2)):
            there = lax.rem(a + 4 + step, 4)
            sender.start(
                total.at[cut(dim, there)], slots.at[p, k], sem + k, place.along(dim, step)
            )
        yield
        for k, step in enumerate((-1, 1, 2)):
            sender.arrived(slots.at[p, k], sem + k, place.along(dim, step))
        i = cut(dim, a)
        value = (total[i] + slots[p, 0]) + (slots[p, 1] + slots[p, 2])
        if phase == 2:
            out_ref[8 * p : 8 * p + 8, :] = value
        else:
            total[i] = value
        where[dim] = a


GROUPS = ((0, 1), (1, 3), (3, 6))


def head_kernel(
    targets_ref, sources_ref, emb_ref, signs_ref, gaussian_ref, scales_ref, phases_ref,
    weights_ref, perms_ref,
    out_ref, line_ref,
    gathered7, places_all, places_ref, perms, emb32, part, first, placed, feats,
    outgoing, theirs, total, wide, narrow, last, lines,
    send, recv, own,
):
    place = Place()
    x, y, z, c, h = place.x, place.y, place.z, place.c, place.h
    partner = place.at(c=1 - c)
    me = ((x * 4 + y) * 2 + z) * 2 + c
    given = [signs_ref, None, gaussian_ref, scales_ref, phases_ref, weights_ref]
    copies = []
    for v, ref in enumerate(given):
        if ref is not None:
            copies.append(pltpu.make_async_copy(ref, gathered7.at[v, x, y, z, c], own.at[v]))
    get_perms = pltpu.make_async_copy(perms_ref, perms, own.at[6])
    for copy in copies:
        copy.start()
    get_perms.start()
    places_all[x, y, z, c, 0:1, 0:64] = sources_ref[...]
    greet(place)
    for copy in copies:
        copy.wait()
    sender = Sender(send, recv)

    def getter(group, quarter):
        vs = slice(*GROUPS[group])

        def get(sel, half):
            rows = pl.ds(16 * quarter, 16) if half is None else pl.ds(16 * quarter + 8 * half, 8)
            return gathered7.at[vs, sel["x"], sel["y"], sel["z"], sel["c"], rows, :]

        return get

    def get_places(sel, half):
        return places_all.at[sel["x"], sel["y"], sel["z"], sel["c"]]

    def get_lines(sel, half):
        return lines.at[sel["x"], sel["y"], sel["z"], sel["c"]]

    groups = []
    for group in range(3):
        groups.append([])
        for q in range(4):
            base = STREAM_SEMS * (4 * group + q)
            groups[group].append(
                gather_stream(place, sender, base, ORDERS[q], getter(group, q), True)
            )
    groups[0].append(gather_stream(place, sender, STREAM_SEMS * 12, "zyx", get_places, False))

    advance(groups[0])
    get_perms.wait()
    lanes = lax.broadcasted_iota(jnp.int32, (8, LANES), 1).astype(F32).astype(BF16)

    def order_of(t, _):
        rows = []
        for q in range(8):
            line = lax.dot_general(
                lanes, perms[8 * t + q], (((1,), (1,)), ((), ())), preferred_element_type=F32
            )
            rows.append(line[0:1])
        gathered7[1, x, y, z, c, pl.ds(pl.multiple_of(8 * t, 8), 8), :] = jnp.concatenate(rows, axis=0)
        return 0

    lax.fori_loop(0, 8, order_of, 0)
    advance(groups[1])
    advance(groups[0])
    advance(groups[2])
    advance(groups[1])
    advance(groups[0])
    advance(groups[2])
    advance(groups[1])
    advance(groups[2])
    gathered = gathered7.reshape(6, N_BLOCKS, LANES)

    h1 = signs_128()
    h2 = jnp.concatenate([h1, h1], axis=0)
    for d in range(4):
        emb32[d] = emb_ref[:, d * LANES : (d + 1) * LANES].astype(F32)
    emb = [[emb32[d, pl.ds(2 * me + r, 1), :] for d in range(4)] for r in range(2)]

    advance(groups[0])
    advance(groups[0])
    to_smem = pltpu.make_async_copy(places_all, places_ref, own.at[7])
    to_smem.start()

    for k_hi in range(8):
        for d in range(4):
            s = gathered[0, pl.ds(512 * k_hi + d, LANES, stride=4), :]
            part[k_hi, d] = jnp.dot(h1, s.astype(BF16), preferred_element_type=F32)

    def stage_u(t, _):
        rows = pl.ds(pl.multiple_of(8 * t, 8), 8)
        cols = []
        for d in range(4):
            cols.append(butterfly([part[k, d, rows, :] for k in range(8)]))
        for k in range(8):
            for r in range(2):
                u = butterfly([emb[r][d] * cols[d][k] for d in range(4)])
                for b in range(4):
                    placed[r, pl.ds(512 * k + 32 * t + b, 8, stride=4), :] = u[b]
        return 0

    lax.fori_loop(0, 16, stage_u, 0)

    for r in range(2):

        def stage_f(t, _, r=r):
            rows = pl.ds(pl.multiple_of(256 * t, 256), 256)
            first[r, rows, :] = times_h(placed[r, rows, :], h2)
            return 0

        lax.fori_loop(0, 16, stage_f, 0)

    advance(groups[1])
    to_smem.wait()

    def stage_g(t, _):
        for q in range(16):
            b = 16 * t + q
            device = t // 4
            s = places_ref[
                device // 16, lax.rem(device // 4, 4), lax.rem(device // 2, 2),
                lax.rem(device, 2), 0, 16 * lax.rem(t, 4) + q,
            ]
            for r in range(2):
                placed[r, pl.ds(b, 1), :] = first[r, pl.ds(s, 1), :]
        return 0

    lax.fori_loop(0, N_BLOCKS // 16, stage_g, 0)
    advance(groups[1])

    def stage_m(t, _):
        xs = [[], []]
        for q in range(16):
            rows = pl.ds(pl.multiple_of(128 * t + 8 * q, 8), 8)
            order = gathered[1, rows, :].astype(jnp.int32)
            g = gathered[2, rows, :]
            for r in range(2):
                xs[r].append(jnp.take_along_axis(placed[r, rows, :], order, axis=1) * g)
        for r in range(2):
            v = times_h(jnp.concatenate(xs[r], axis=0), h2)
            v = butterfly([v[8 * q : 8 * q + 8] for q in range(16)])
            for q in range(16):
                first[r, pl.ds(pl.multiple_of(128 * t + 8 * q, 8), 8), :] = v[q]
        return 0

    lax.fori_loop(0, 32, stage_m, 0)
    advance(groups[2])

    def stage_b(t, _):
        rows = [pl.ds(pl.multiple_of(128 * k + 8 * t, 8), 8) for k in range(32)]
        for r in range(2):
            v = butterfly([first[r, rows[k], :] for k in range(32)])
            for k in range(32):
                first[r, rows[k], :] = v[k]
        return 0

    lax.fori_loop(0, 16, stage_b, 0)
    advance(groups[2])

    def stage_c(t, acc):
        rows = [pl.ds(64 * t + s, 8, stride=8) for s in range(8)]
        ys = [butterfly([first[r, rows[s], :] for s in range(8)]) for r in range(2)]
        acc = list(acc)
        for s in range(8):
            scale = gathered[3, rows[s], :] * (1.0 / FEATURE_COUNT)
            phase = gathered[4, rows[s], :]
            weight = gathered[5, rows[s], :]
            for r in range(2):
                f = cosine(scale * ys[r][s] + phase)
                feats[r, rows[s], :] = f
                acc[r] = acc[r] + f * weight
        return tuple(acc)

    zero = jnp.zeros((8, LANES), F32)
    acc = lax.fori_loop(0, 64, stage_c, (zero, zero))
    line = jnp.zeros((1, LANES), F32)
    lane = lax.broadcasted_iota(jnp.int32, (1, LANES), 1)
    residual = []
    for r in range(2):
        p = jnp.sum(acc[r], axis=(0, 1), keepdims=True) * (1.0 / math.sqrt(FEATURE_COUNT))
        line = jnp.where(lane == 2 * me + r, p, line)
        residual.append((p - targets_ref[2 * me + r]) * (1.0 / 16.0))
    lines[x, y, z, c] = line

    def gradients(p, core, t):
        row = (t // 4) * 256 + lax.rem(t, 2) * 128 + core * 64 + lax.rem(t // 2, 2) * 32 + 8 * p
        rows = pl.ds(pl.multiple_of(row, 8), 8)
        return feats[0, rows, :] * residual[0] + feats[1, rows, :] * residual[1]

    base = STREAM_SEMS * 13
    for p in range(4):

        def stage_o(t, _, p=p):
            for q in range(4):
                i = 4 * t + q
                outgoing[p, t // 4, lax.rem(t, 4), q] = gradients(p, 1 - c, i)
            return 0

        lax.fori_loop(0, 16, stage_o, 0)
        sender.start(outgoing.at[p], theirs.at[p], base + 10 * p, partner)

    def part_stream(p):
        sender.arrived(theirs.at[p], base + 10 * p, partner)

        def stage_s(t, _):
            for q in range(4):
                i = 4 * t + q
                at = (p, t // 4, lax.rem(t, 4), q)
                total[at] = gradients(p, c, i) + theirs[at]
            return 0

        lax.fori_loop(0, 16, stage_s, 0)
        yield from reduce_part(
            place, sender, base + 10 * p + 1, p, REDUCE_ORDERS[p], total, wide, narrow, last, out_ref
        )

    line_stream = gather_stream(place, sender, base + 40, "zyx", get_lines, False)
    run_streams([part_stream(p) for p in range(4)] + [line_stream])
    line = jnp.zeros((1, LANES), F32)
    for i in range(64):
        line = line + lines[i // 16, (i // 4) % 4, (i // 2) % 2, i % 2]
    line_ref[...] = line
    sender.finish()


N_SEMS = STREAM_SEMS * 13 + 40 + STREAM_SEMS


def local(
    embeddings,
    sign_flips,
    gaussian,
    scales,
    phases,
    source_blocks,
    block_permutations,
    weights,
    targets,
):
    rows = lambda v: v.reshape(-1, LANES)
    vmem = pl.BlockSpec(memory_space=pltpu.VMEM)
    smem = pl.BlockSpec(memory_space=pltpu.SMEM)
    any_ = pl.BlockSpec(memory_space=pl.ANY)
    field = pltpu.VMEM((2, N_BLOCKS, LANES), F32)
    tiles = lambda *shape: pltpu.VMEM(shape + (8, LANES), F32)
    grad_out, line = pl.pallas_call(
        head_kernel,
        out_shape=(
            jax.ShapeDtypeStruct((32, LANES), F32),
            jax.ShapeDtypeStruct((1, LANES), F32),
        ),
        in_specs=[smem, vmem, vmem] + [any_] * 6,
        out_specs=(vmem, vmem),
        scratch_shapes=[
            pltpu.VMEM((6, 4, 4, 2, 2, 64, LANES), F32),
            pltpu.VMEM((4, 4, 2, 2, 1, LANES), jnp.int32),
            pltpu.SMEM((4, 4, 2, 2, 1, LANES), jnp.int32),
            pltpu.VMEM((64, LANES, LANES), BF16),
            pltpu.VMEM((4, 128, LANES), F32),
            pltpu.VMEM((8, 4, LANES, LANES), F32),
            field, field, field,
            tiles(4, 4, 4, 4), tiles(4, 4, 4, 4), tiles(4, 4, 4, 4),
            tiles(4, 3, 4, 4), tiles(4, 3, 4), tiles(4, 3),
            pltpu.VMEM((4, 4, 2, 2, 1, LANES), F32),
            pltpu.SemaphoreType.DMA((N_SEMS,)),
            pltpu.SemaphoreType.DMA((N_SEMS,)),
            pltpu.SemaphoreType.DMA((8,)),
        ],
        compiler_params=pltpu.CompilerParams(
            vmem_limit_bytes=60 * 2**20, collective_id=0, has_side_effects=True
        ),
    )(
        targets, source_blocks.reshape(1, -1), embeddings, rows(sign_flips), rows(gaussian),
        rows(scales), rows(phases), rows(weights), block_permutations,
    )
    return line.reshape(-1), grad_out.reshape(-1)


def solution(mesh):
    in_specs = (
        P("rows", None), P("feat"), P("feat"), P("feat"), P("feat"), P("feat"),
        P("feat", None, None), P("feat"), P("rows"),
    )
    out_specs = (P("rows"), P(("feat", "rows")))
    return jax.shard_map(local, mesh=mesh, in_specs=in_specs, out_specs=out_specs, check_vma=False)
```

time: 491 us -> 109 us (0.22)
  blocking collectives: 422 us -> 0 us
  Pallas kernels: 40.4 us -> 105 us
  between operations: 15.5 us -> 0.64 us
  waiting for transfers between devices: 7.44 us -> 0 us
    unnamed x1 -> x0, blocking collectives: 277 us -> none
    all_gather x1 -> x0, blocking collectives: 145 us -> none  [local(): predictions = lax.all_gather(preds[:, 0, 0], 'feat', tiled=True)]
    pallas_call x1, Pallas kernels: 40.4 us -> 105 us  [local(): pl.pallas_call(head_kernel, out_shape=(jax.ShapeDtypeStruct((32, LANES),...]
    unnamed x3 -> x0, waiting for transfers between devices: 7.44 us -> none
  transfers between devices with their start and end apart: 2 -> 0, of which waited for: 1 -> 0; matrix products, arithmetic and copies ran while one was open for 0% -> 0% of each run, Pallas kernels for 0% -> 0%
where the time goes in v3:
time: 109 us; the launch traced here: 108 us
  Pallas kernels  105 us (96%)
  local copies, waits for them, and re-layouts  2.46 us (2%)
    pallas_call x1, Pallas kernels, local(): pl.pallas_call(head_kernel, out_shape=(jax.ShapeDtypeStruct((32, LANES),...  105 us
    unnamed x2, local copies, waits for them, and re-layouts  2.46 us

profile of v3, /device:TPU:1, one launch (start us, length us, event | category | flops | bytes accessed | tf_op | source)
XLA Modules:
  0.0 108.3 jit_solution(12349163960957886573)
XLA Ops:
  0.6 105.2 %shard_map.104 = (f32[32,128]{1,0:T(8,128)}, f32[1,128]{1,0:T(1,128)}) custom-call(f32[128]{0:T(128)} %targets_ref.1, s32[1,64]{1,0:T(1,128)} %bitcast.14, bf16[128,512]{1,0:T(8,128)(2,1)} %emb_ref.1, f32[64,128]{1,0:T(8,128)} %bitcast.8, f32[64,128]{1,0:T(8,128)} %bitcast.9, f32[64,128]{1,0:T(8,128)} %bitcast.10, f32[64,128]{1,0:T(8,128)} %bitcast.11, ...), custom_call_target="tpu_custom_call" | custom-call | tf_op jit(solution)/shard_map/pallas_call | solution.py:499
  105.9 1.1 %copy.13 = f32[128]{0:T(128)} copy(f32[128]{0:T(128)} %bitcast.15) | data formatting | bytes 1024
  107.0 1.3 %copy.14 = f32[4096]{0:T(1024)} copy(f32[4096]{0:T(1024)} %bitcast.13) | data formatting | bytes 32768

commit v4 on v3

--- a/solution.py
+++ b/solution.py
@@ -77,7 +77,7 @@
 
 MESH = pl.DeviceIdType.MESH
 ALL = slice(None)
-ORDERS = ("zyx", "zxy", "yxz", "xyz")
+ORDERS = ("yzx", "xzy", "xyz", "yxz")
 STREAM_SEMS = 14
 DIMS = ("x", "y", "zz")
 
@@ -117,6 +117,17 @@
     for device in others:
         pl.semaphore_signal(barrier, inc=1, device_id=device, device_id_type=MESH)
     pl.semaphore_wait(barrier, len(others))
+
+
+PLAN = (
+    0, 2, 3, 4, "order", 1,
+    0, 1, 0, 2, 3, 4, 1, 2, 3, 4,
+    0, 0, "t", "f", ("g", 0, 64),
+    1, 1, ("m", 0, 16),
+    2, ("m", 16, 32),
+    3, ("b", 0, 16),
+    4, 2, 3, ("c", 0, 64), 4,
+)
 
 
 class Sender:
@@ -208,43 +219,53 @@
         next(s, None)
 
 
-REDUCE_ORDERS = (("x", "y", "zz"), ("y", "zz", "x"), ("zz", "x", "y"), ("zz", "y", "x"))
-
-
-def reduce_part(place, sender, base, p, order, total, wide, narrow, last, out_ref):
-    where = {d: None for d in DIMS}
-
-    def cut(dim, index):
-        parts = []
-        for d in DIMS:
-            if d == dim:
-                parts.append(index)
-            else:
-                parts.append(ALL if where[d] is None else where[d])
-        return (p, *parts)
-
-    for phase, dim in enumerate(order):
-        a = getattr(place, dim)
-        slots = (wide, narrow, last)[phase]
-        sem = base + 3 * phase
+class Reducer:
+    def __init__(self, place, sender, total):
+        self.place, self.sender, self.total = place, sender, total
+
+    def entry(self, p, sel, dim, a):
+        here = {**sel, "z": lax.rem(a, 2), "h": a // 2} if dim == "zz" else {**sel, dim: a}
+        return (p, *(here[d] for d in "xyzh"))
+
+    def start(self, p, sel, dim, slots, sem):
+        a = getattr(self.place, dim)
         for k, step in enumerate((1, -1, 2)):
             there = lax.rem(a + 4 + step, 4)
-            sender.start(
-                total.at[cut(dim, there)], slots.at[p, k], sem + k, place.along(dim, step)
+            self.sender.start(
+                self.total.at[self.entry(p, sel, dim, there)], slots.at[k], sem + k,
+                self.place.along(dim, step),
             )
-        yield
+
+    def finish(self, p, sel, dim, slots, sem):
         for k, step in enumerate((-1, 1, 2)):
-            sender.arrived(slots.at[p, k], sem + k, place.along(dim, step))
-        i = cut(dim, a)
-        value = (total[i] + slots[p, 0]) + (slots[p, 1] + slots[p, 2])
-        if phase == 2:
-            out_ref[8 * p : 8 * p + 8, :] = value
-        else:
-            total[i] = value
-        where[dim] = a
-
-
-GROUPS = ((0, 1), (1, 3), (3, 6))
+            self.sender.arrived(slots.at[k], sem + k, self.place.along(dim, step))
+        i = self.entry(p, sel, dim, getattr(self.place, dim))
+        value = (self.total[i] + slots[0]) + (slots[1] + slots[2])
+        self.total[i] = value
+        return i, value
+
+    def pinned(self, dim):
+        if dim == "zz":
+            return {"z": self.place.z, "h": self.place.h}
+        return {dim: getattr(self.place, dim)}
+
+    def rings(self, p, sel, order, slots, sem):
+        for dim, slot in zip(order, slots):
+            self.start(p, sel, dim, slot, sem)
+            yield
+            value = self.finish(p, sel, dim, slot, sem)[1]
+            sel = {**sel, **self.pinned(dim)}
+            sem += 3
+        return value
+
+
+def reduce_scratch():
+    shapes = [(4, 2, 2), (2, 2), (), (4, 2, 2), (4,), (), (4, 4), (4,), ()]
+    shapes += [(4, 2), (2,), (4, 2), (2,), ()]
+    return [pltpu.VMEM((3,) + shape + (8, LANES), F32) for shape in shapes]
+
+
+GROUPS = ((0, 1), (1, 3), (3, 4), (4, 5), (5, 6))
 
 
 def head_kernel(
@@ -252,8 +273,8 @@
     weights_ref, perms_ref,
     out_ref, line_ref,
     gathered7, places_all, places_ref, perms, emb32, part, first, placed, feats,
-    outgoing, theirs, total, wide, narrow, last, lines,
-    send, recv, own,
+    outgoing, theirs, total, lines,
+    send, recv, own, *slots,
 ):
     place = Place()
     x, y, z, c, h = place.x, place.y, place.z, place.c, place.h
@@ -290,18 +311,24 @@
         return lines.at[sel["x"], sel["y"], sel["z"], sel["c"]]
 
     groups = []
-    for group in range(3):
+    for group in range(len(GROUPS)):
         groups.append([])
         for q in range(4):
             base = STREAM_SEMS * (4 * group + q)
             groups[group].append(
                 gather_stream(place, sender, base, ORDERS[q], getter(group, q), True)
             )
-    groups[0].append(gather_stream(place, sender, STREAM_SEMS * 12, "zyx", get_places, False))
-
-    advance(groups[0])
-    get_perms.wait()
+    groups[0].append(gather_stream(place, sender, STREAM_SEMS * 4 * len(GROUPS), "zyx", get_places, False))
+
     lanes = lax.broadcasted_iota(jnp.int32, (8, LANES), 1).astype(F32).astype(BF16)
+
+    gathered = gathered7.reshape(6, N_BLOCKS, LANES)
+
+    h1 = signs_128()
+    h2 = jnp.concatenate([h1, h1], axis=0)
+    for d in range(4):
+        emb32[d] = emb_ref[:, d * LANES : (d + 1) * LANES].astype(F32)
+    emb = [[emb32[d, pl.ds(2 * me + r, 1), :] for d in range(4)] for r in range(2)]
 
     def order_of(t, _):
         rows = []
@@ -313,32 +340,11 @@
         gathered7[1, x, y, z, c, pl.ds(pl.multiple_of(8 * t, 8), 8), :] = jnp.concatenate(rows, axis=0)
         return 0
 
-    lax.fori_loop(0, 8, order_of, 0)
-    advance(groups[1])
-    advance(groups[0])
-    advance(groups[2])
-    advance(groups[1])
-    advance(groups[0])
-    advance(groups[2])
-    advance(groups[1])
-    advance(groups[2])
-    gathered = gathered7.reshape(6, N_BLOCKS, LANES)
-
-    h1 = signs_128()
-    h2 = jnp.concatenate([h1, h1], axis=0)
-    for d in range(4):
-        emb32[d] = emb_ref[:, d * LANES : (d + 1) * LANES].astype(F32)
-    emb = [[emb32[d, pl.ds(2 * me + r, 1), :] for d in range(4)] for r in range(2)]
-
-    advance(groups[0])
-    advance(groups[0])
-    to_smem = pltpu.make_async_copy(places_all, places_ref, own.at[7])
-    to_smem.start()
-
-    for k_hi in range(8):
-        for d in range(4):
-            s = gathered[0, pl.ds(512 * k_hi + d, LANES, stride=4), :]
-            part[k_hi, d] = jnp.dot(h1, s.astype(BF16), preferred_element_type=F32)
+    def stage_t():
+        for k_hi in range(8):
+            for d in range(4):
+                s = gathered[0, pl.ds(512 * k_hi + d, LANES, stride=4), :]
+                part[k_hi, d] = jnp.dot(h1, s.astype(BF16), preferred_element_type=F32)
 
     def stage_u(t, _):
         rows = pl.ds(pl.multiple_of(8 * t, 8), 8)
@@ -352,34 +358,18 @@
                     placed[r, pl.ds(512 * k + 32 * t + b, 8, stride=4), :] = u[b]
         return 0
 
-    lax.fori_loop(0, 16, stage_u, 0)
-
-    for r in range(2):
-
-        def stage_f(t, _, r=r):
-            rows = pl.ds(pl.multiple_of(256 * t, 256), 256)
+    def stage_f(t, _):
+        rows = pl.ds(pl.multiple_of(256 * t, 256), 256)
+        for r in range(2):
             first[r, rows, :] = times_h(placed[r, rows, :], h2)
-            return 0
-
-        lax.fori_loop(0, 16, stage_f, 0)
-
-    advance(groups[1])
-    to_smem.wait()
+        return 0
 
     def stage_g(t, _):
-        for q in range(16):
-            b = 16 * t + q
-            device = t // 4
-            s = places_ref[
-                device // 16, lax.rem(device // 4, 4), lax.rem(device // 2, 2),
-                lax.rem(device, 2), 0, 16 * lax.rem(t, 4) + q,
-            ]
+        for q in range(64):
+            s = places_ref[t, 0, q]
             for r in range(2):
-                placed[r, pl.ds(b, 1), :] = first[r, pl.ds(s, 1), :]
-        return 0
-
-    lax.fori_loop(0, N_BLOCKS // 16, stage_g, 0)
-    advance(groups[1])
+                placed[r, pl.ds(64 * t + q, 1), :] = first[r, pl.ds(s, 1), :]
+        return 0
 
     def stage_m(t, _):
         xs = [[], []]
@@ -396,9 +386,6 @@
                 first[r, pl.ds(pl.multiple_of(128 * t + 8 * q, 8), 8), :] = v[q]
         return 0
 
-    lax.fori_loop(0, 32, stage_m, 0)
-    advance(groups[2])
-
     def stage_b(t, _):
         rows = [pl.ds(pl.multiple_of(128 * k + 8 * t, 8), 8) for k in range(32)]
         for r in range(2):
@@ -407,25 +394,50 @@
                 first[r, rows[k], :] = v[k]
         return 0
 
-    lax.fori_loop(0, 16, stage_b, 0)
-    advance(groups[2])
-
-    def stage_c(t, acc):
+    def stage_c(t, _):
         rows = [pl.ds(64 * t + s, 8, stride=8) for s in range(8)]
         ys = [butterfly([first[r, rows[s], :] for s in range(8)]) for r in range(2)]
-        acc = list(acc)
         for s in range(8):
             scale = gathered[3, rows[s], :] * (1.0 / FEATURE_COUNT)
             phase = gathered[4, rows[s], :]
-            weight = gathered[5, rows[s], :]
             for r in range(2):
-                f = cosine(scale * ys[r][s] + phase)
-                feats[r, rows[s], :] = f
-                acc[r] = acc[r] + f * weight
-        return tuple(acc)
+                feats[r, rows[s], :] = cosine(scale * ys[r][s] + phase)
+        return 0
+
+    def stage_d(t, acc):
+        out = []
+        rows = [pl.ds(pl.multiple_of(128 * t + 8 * q, 8), 8) for q in range(16)]
+        weight = [gathered[5, rows[q], :] for q in range(16)]
+        for r in range(2):
+            v = [feats[r, rows[q], :] * weight[q] for q in range(16)]
+            while len(v) > 1:
+                v = [v[k] + v[k + 1] for k in range(0, len(v), 2)]
+            out.append(acc[r] + v[0])
+        return tuple(out)
+
+    to_smem = pltpu.make_async_copy(places_all.reshape(64, 1, LANES), places_ref, own.at[7])
+    for step in PLAN:
+        if isinstance(step, int):
+            advance(groups[step])
+        elif step == "order":
+            get_perms.wait()
+            lax.fori_loop(0, 8, order_of, 0)
+        elif step == "t":
+            to_smem.start()
+            stage_t()
+            lax.fori_loop(0, 16, stage_u, 0, unroll=2)
+        elif step == "f":
+            lax.fori_loop(0, 16, stage_f, 0, unroll=8)
+            to_smem.wait()
+        else:
+            stage, low, high = step
+            loop, unroll = {
+                "g": (stage_g, 1), "m": (stage_m, 4), "b": (stage_b, 1), "c": (stage_c, 4)
+            }[stage]
+            lax.fori_loop(low, high, loop, 0, unroll=unroll)
 
     zero = jnp.zeros((8, LANES), F32)
-    acc = lax.fori_loop(0, 64, stage_c, (zero, zero))
+    acc = lax.fori_loop(0, 32, stage_d, (zero, zero))
     line = jnp.zeros((1, LANES), F32)
     lane = lax.broadcasted_iota(jnp.int32, (1, LANES), 1)
     residual = []
@@ -436,39 +448,67 @@
     lines[x, y, z, c] = line
 
     def gradients(p, core, t):
-        row = (t // 4) * 256 + lax.rem(t, 2) * 128 + core * 64 + lax.rem(t // 2, 2) * 32 + 8 * p
-        rows = pl.ds(pl.multiple_of(row, 8), 8)
-        return feats[0, rows, :] * residual[0] + feats[1, rows, :] * residual[1]
-
-    base = STREAM_SEMS * 13
+        out = []
+        for i in range(16):
+            row = 1024 * t + (i // 4) * 256 + ((i // 2) % 2) * 128 + (i % 2) * 32 + 8 * p + core * 64
+            rows = pl.ds(pl.multiple_of(row, 8), 8)
+            out.append(feats[0, rows, :] * residual[0] + feats[1, rows, :] * residual[1])
+        return out
+
     for p in range(4):
 
         def stage_o(t, _, p=p):
-            for q in range(4):
-                i = 4 * t + q
-                outgoing[p, t // 4, lax.rem(t, 4), q] = gradients(p, 1 - c, i)
+            for i, value in enumerate(gradients(p, 1 - c, t)):
+                outgoing[p, t, i // 4, (i // 2) % 2, i % 2] = value
             return 0
 
-        lax.fori_loop(0, 16, stage_o, 0)
-        sender.start(outgoing.at[p], theirs.at[p], base + 10 * p, partner)
-
-    def part_stream(p):
-        sender.arrived(theirs.at[p], base + 10 * p, partner)
+        lax.fori_loop(0, 4, stage_o, 0, unroll=2)
+        sender.start(outgoing.at[p], theirs.at[p], REDUCE_BASE + p, partner)
+
+    reducer = Reducer(place, sender, total)
+    whole = {d: ALL for d in "xyzh"}
+
+    def add_theirs(p):
+        sender.arrived(theirs.at[p], REDUCE_BASE + p, partner)
 
         def stage_s(t, _):
-            for q in range(4):
-                i = 4 * t + q
-                at = (p, t // 4, lax.rem(t, 4), q)
-                total[at] = gradients(p, c, i) + theirs[at]
+            values = gradients(p, c, t)
+            values = [v + theirs[p, t, i // 4, (i // 2) % 2, i % 2] for i, v in enumerate(values)]
+            for i, value in enumerate(values):
+                total[p, t, i // 4, (i // 2) % 2, i % 2] = value
             return 0
 
-        lax.fori_loop(0, 16, stage_s, 0)
-        yield from reduce_part(
-            place, sender, base + 10 * p + 1, p, REDUCE_ORDERS[p], total, wide, narrow, last, out_ref
-        )
-
-    line_stream = gather_stream(place, sender, base + 40, "zyx", get_lines, False)
-    run_streams([part_stream(p) for p in range(4)] + [line_stream])
+        lax.fori_loop(0, 4, stage_s, 0, unroll=2)
+
+    def part_stream(p, order, sem):
+        add_theirs(p)
+        value = yield from reducer.rings(p, whole, order, slots[3 * p : 3 * p + 3], sem)
+        out_ref[8 * p : 8 * p + 8, :] = value
+
+    def last_stream(sem):
+        add_theirs(3)
+        halves = [
+            reducer.rings(3, {**whole, "z": k}, order, slots[9 + 2 * k : 11 + 2 * k], sem + 6 * k)
+            for k, order in enumerate((("x", "y"), ("y", "x")))
+        ]
+        for _ in range(3):
+            advance(halves)
+            if _ < 2:
+                yield
+        sel = {**whole, "x": x, "y": y}
+        value = yield from reducer.rings(3, sel, ("zz",), slots[13:14], sem + 12)
+        out_ref[24:32, :] = value
+
+    sem = REDUCE_BASE + 4
+    run_streams(
+        [
+            part_stream(0, ("x", "y", "zz"), sem),
+            part_stream(1, ("y", "zz", "x"), sem + 9),
+            part_stream(2, ("zz", "x", "y"), sem + 18),
+            last_stream(sem + 27),
+            gather_stream(place, sender, REDUCE_BASE + 50, "zyx", get_lines, False),
+        ]
+    )
     line = jnp.zeros((1, LANES), F32)
     for i in range(64):
         line = line + lines[i // 16, (i // 4) % 4, (i // 2) % 2, i % 2]
@@ -476,7 +516,8 @@
     sender.finish()
 
 
-N_SEMS = STREAM_SEMS * 13 + 40 + STREAM_SEMS
+REDUCE_BASE = STREAM_SEMS * (4 * len(GROUPS) + 1)
+N_SEMS = REDUCE_BASE + 50 + STREAM_SEMS
 
 
 def local(
@@ -507,17 +548,17 @@
         scratch_shapes=[
             pltpu.VMEM((6, 4, 4, 2, 2, 64, LANES), F32),
             pltpu.VMEM((4, 4, 2, 2, 1, LANES), jnp.int32),
-            pltpu.SMEM((4, 4, 2, 2, 1, LANES), jnp.int32),
+            pltpu.SMEM((64, 1, LANES), jnp.int32),
             pltpu.VMEM((64, LANES, LANES), BF16),
             pltpu.VMEM((4, 128, LANES), F32),
             pltpu.VMEM((8, 4, LANES, LANES), F32),
             field, field, field,
-            tiles(4, 4, 4, 4), tiles(4, 4, 4, 4), tiles(4, 4, 4, 4),
-            tiles(4, 3, 4, 4), tiles(4, 3, 4), tiles(4, 3),
+            tiles(4, 4, 4, 2, 2), tiles(4, 4, 4, 2, 2), tiles(4, 4, 4, 2, 2),
             pltpu.VMEM((4, 4, 2, 2, 1, LANES), F32),
             pltpu.SemaphoreType.DMA((N_SEMS,)),
             pltpu.SemaphoreType.DMA((N_SEMS,)),
             pltpu.SemaphoreType.DMA((8,)),
+            *reduce_scratch(),
         ],
         compiler_params=pltpu.CompilerParams(
             vmem_limit_bytes=60 * 2**20, collective_id=0, has_side_effects=True

time: 109 us -> 79.6 us (0.73)
  Pallas kernels: 105 us -> 76.3 us
    pallas_call x1, Pallas kernels: 105 us -> 76.3 us  [local(): pl.pallas_call(head_kernel, out_shape=(jax.ShapeDtypeStruct((32, LANES),...]
where the time goes in v4:
time: 79.6 us; the launch traced here: 79.4 us
  Pallas kernels  76.3 us (96%)
  local copies, waits for them, and re-layouts  2.46 us (3%)
    pallas_call x1, Pallas kernels, local(): pl.pallas_call(head_kernel, out_shape=(jax.ShapeDtypeStruct((32, LANES),...  76.3 us
    unnamed x2, local copies, waits for them, and re-layouts  2.46 us

profile of v4, /device:TPU:1, one launch (start us, length us, event | category | flops | bytes accessed | tf_op | source)
XLA Modules:
  0.0 79.4 jit_solution(13971274339081495225)
XLA Ops:
  0.6 76.3 %shard_map.104 = (f32[32,128]{1,0:T(8,128)}, f32[1,128]{1,0:T(1,128)}) custom-call(f32[128]{0:T(128)} %targets_ref.1, s32[1,64]{1,0:T(1,128)} %bitcast.14, bf16[128,512]{1,0:T(8,128)(2,1)} %emb_ref.1, f32[64,128]{1,0:T(8,128)} %bitcast.8, f32[64,128]{1,0:T(8,128)} %bitcast.9, f32[64,128]{1,0:T(8,128)} %bitcast.10, f32[64,128]{1,0:T(8,128)} %bitcast.11, ...), custom_call_target="tpu_custom_call" | custom-call | tf_op jit(solution)/shard_map/pallas_call | solution.py:540
  76.9 1.1 %copy.13 = f32[128]{0:T(128)} copy(f32[128]{0:T(128)} %bitcast.15) | data formatting | bytes 1024
  78.0 1.3 %copy.14 = f32[4096]{0:T(1024)} copy(f32[4096]{0:T(1024)} %bitcast.13) | data formatting | bytes 32768

commit v5 on v4

--- a/solution.py
+++ b/solution.py
@@ -78,6 +78,7 @@
 MESH = pl.DeviceIdType.MESH
 ALL = slice(None)
 ORDERS = ("yzx", "xzy", "xyz", "yxz")
+RELAYED = (2,)
 STREAM_SEMS = 14
 DIMS = ("x", "y", "zz")
 
@@ -120,13 +121,14 @@
 
 
 PLAN = (
-    0, 2, 3, 4, "order", 1,
-    0, 1, 0, 2, 3, 4, 1, 2, 3, 4,
-    0, 0, "t", "f", ("g", 0, 64),
-    1, 1, ("m", 0, 16),
-    2, ("m", 16, 32),
-    3, ("b", 0, 16),
-    4, 2, 3, ("c", 0, 64), 4,
+    0, 2, 3, "order", 1,
+    0, 1, 0, 2, 3, 0, 1, 0, 0, "t",
+    1, 2, 3, "f", ("g", 0, 32),
+    1, ("g", 32, 64),
+    2, 1, ("m", 0, 16),
+    3, 2, ("m", 16, 32),
+    ("b", 0, 16),
+    2, 3, ("c", 0, 64), 3,
 )
 
 
@@ -165,6 +167,7 @@
         sender.start(here, here, index, partner)
         mirrored.append((get({**sel, **where, "c": 1 - place.c}, None), index))
 
+    relays = 0
     for phase, dim in enumerate(order):
         final = phase == 2
         if dim == "z":
@@ -181,6 +184,32 @@
             if final:
                 mirror(base + 11, z=other)
             sem += 2
+        elif halves and phase in RELAYED:
+            relays += 1
+            a = sel[dim]
+            up, down = place.along(dim, 1), place.along(dim, -1)
+            below, above, across = (lax.rem(a + k, 4) for k in (3, 1, 2))
+            own = get(sel, None)
+            sender.start(own, own, sem, up)
+            sender.start(own, own, sem + 1, down)
+            if final:
+                mirror(base + 10)
+            yield
+            sender.arrived(get({**sel, dim: below}, None), sem, down)
+            ref = get({**sel, dim: below}, 0)
+            sender.start(ref, ref, sem + 2, up)
+            sender.arrived(get({**sel, dim: above}, None), sem + 1, up)
+            ref = get({**sel, dim: above}, 1)
+            sender.start(ref, ref, sem + 3, down)
+            if final:
+                mirror(base + 11, **{dim: below})
+                mirror(base + 12, **{dim: above})
+            yield
+            sender.arrived(get({**sel, dim: across}, 0), sem + 2, down)
+            sender.arrived(get({**sel, dim: across}, 1), sem + 3, up)
+            if final:
+                mirror(base + 13, **{dim: across})
+            sem += 4
         else:
             a = sel[dim]
             own = get(sel, None)
@@ -197,6 +226,8 @@
             sem += 3
         sel[dim] = ALL
     yield
+    if relays == 0 and RELAYED:
+        yield
     for ref, index in mirrored:
         sender.arrived(ref, index, partner)
 
@@ -265,7 +296,7 @@
     return [pltpu.VMEM((3,) + shape + (8, LANES), F32) for shape in shapes]
 
 
-GROUPS = ((0, 1), (1, 3), (3, 4), (4, 5), (5, 6))
+GROUPS = ((0, 1), (1, 3), (3, 5), (5, 6))
 
 
 def head_kernel(
@@ -567,6 +598,20 @@
         targets, source_blocks.reshape(1, -1), embeddings, rows(sign_flips), rows(gaussian),
         rows(scales), rows(phases), rows(weights), block_permutations,
     )
+
+    def hand_over(grad_ref, line_ref, grad_to, line_to):
+        grad_to[...] = grad_ref[...]
+        line_to[...] = line_ref[...]
+
+    grad_out, line = pl.pallas_call(
+        hand_over,
+        out_shape=(
+            jax.ShapeDtypeStruct((32, LANES), F32),
+            jax.ShapeDtypeStruct((1, LANES), F32),
+        ),
+        in_specs=[vmem, vmem],
+        out_specs=(vmem, vmem),
+    )(grad_out, line)
     return line.reshape(-1), grad_out.reshape(-1)
 
 

time: 79.6 us -> 74.9 us (0.941)
  local copies, waits for them, and re-layouts: 2.46 us -> 0 us
  Pallas kernels: 76.3 us -> 74.1 us
    pallas_call x1, Pallas kernels: 76.3 us -> 72.8 us  [local(): pl.pallas_call(head_kernel, out_shape=(jax.ShapeDtypeStruct((32, LANES),...]
    unnamed x2 -> x0, local copies, waits for them, and re-layouts: 2.46 us -> none
    pallas_call x0 -> x1, Pallas kernels: none -> 1.33 us  [local(): pl.pallas_call(hand_over, out_shape=(jax.ShapeDtypeStruct((32, LANES), F3...]
where the time goes in v5:
time: 74.9 us; the launch traced here: 74.7 us
  Pallas kernels  74.1 us (99%)
    pallas_call x1, Pallas kernels, local(): pl.pallas_call(head_kernel, out_shape=(jax.ShapeDtypeStruct((32, LANES),...  72.8 us

profile of v5, /device:TPU:1, one launch (start us, length us, event | category | flops | bytes accessed | tf_op | source)
XLA Modules:
  0.0 74.7 jit_solution(18133834991745627451)
XLA Ops:
  0.6 72.8 %shard_map.104 = (f32[32,128]{1,0:T(8,128)}, f32[1,128]{1,0:T(1,128)}) custom-call(f32[128]{0:T(128)} %targets_ref.1, s32[1,64]{1,0:T(1,128)} %bitcast.13, bf16[128,512]{1,0:T(8,128)(2,1)} %emb_ref.1, f32[64,128]{1,0:T(8,128)} %bitcast.8, f32[64,128]{1,0:T(8,128)} %bitcast.9, f32[64,128]{1,0:T(8,128)} %bitcast.10, f32[64,128]{1,0:T(8,128)} %bitcast.11, ...), custom_call_target="tpu_custom_call" | custom-call | tf_op jit(solution)/shard_map/pallas_call | solution.py:571
  73.4 1.3 %shard_map.105 = (f32[32,128]{1,0:T(8,128)}, f32[1,128]{1,0:T(1,128)}) custom-call(f32[32,128]{1,0:T(8,128)} %get-tuple-element.6.grad_ref, f32[1,128]{1,0:T(1,128)} %get-tuple-element.7.line_ref), custom_call_target="tpu_custom_call" | custom-call | tf_op jit(solution)/shard_map/pallas_call | solution.py:606

commit v6 on v5

--- a/solution.py
+++ b/solution.py
@@ -47,10 +47,6 @@
     return values
 
 
-TWO_PI_A = 6.28125
-TWO_PI_B = 2.0 * math.pi - 6.28125
-
-
 def cos_coefficients():
     import numpy as np
 
@@ -59,15 +55,14 @@
     u = 0.5 * math.pi**2 * (1.0 + np.cos((k + 0.5) * math.pi / n)) * 1.01
     v = np.stack([u**p for p in range(n)], axis=1)
     c = np.linalg.solve(v, np.cos(np.sqrt(u)))
-    return [float(x) for x in c]
+    return [float(x * (2.0 * math.pi) ** (2 * p)) for p, x in enumerate(c)]
 
 
 COS = cos_coefficients()
 
 
-def cosine(x):
-    n = jnp.round(x * (1.0 / (2.0 * math.pi)))
-    r = (x - n * TWO_PI_A) - n * TWO_PI_B
+def cosine_of_turns(t):
+    r = t - jnp.round(t)
     u = r * r
     acc = COS[-1] * u + COS[-2]
     for c in COS[-3::-1]:
@@ -429,10 +424,10 @@
         rows = [pl.ds(64 * t + s, 8, stride=8) for s in range(8)]
         ys = [butterfly([first[r, rows[s], :] for s in range(8)]) for r in range(2)]
         for s in range(8):
-            scale = gathered[3, rows[s], :] * (1.0 / FEATURE_COUNT)
-            phase = gathered[4, rows[s], :]
+            scale = gathered[3, rows[s], :] * (1.0 / (2.0 * math.pi * FEATURE_COUNT))
+            phase = gathered[4, rows[s], :] * (1.0 / (2.0 * math.pi))
             for r in range(2):
-                feats[r, rows[s], :] = cosine(scale * ys[r][s] + phase)
+                feats[r, rows[s], :] = cosine_of_turns(scale * ys[r][s] + phase)
         return 0
 
     def stage_d(t, acc):
@@ -463,7 +458,7 @@
         else:
             stage, low, high = step
             loop, unroll = {
-                "g": (stage_g, 1), "m": (stage_m, 4), "b": (stage_b, 1), "c": (stage_c, 4)
+                "g": (stage_g, 1), "m": (stage_m, 8), "b": (stage_b, 1), "c": (stage_c, 8)
             }[stage]
             lax.fori_loop(low, high, loop, 0, unroll=unroll)
 
@@ -477,6 +472,8 @@
         line = jnp.where(lane == 2 * me + r, p, line)
         residual.append((p - targets_ref[2 * me + r]) * (1.0 / 16.0))
     lines[x, y, z, c] = line
+    line_stream = gather_stream(place, sender, REDUCE_BASE + 50, "zyx", get_lines, False)
+    next(line_stream)
 
     def gradients(p, core, t):
         out = []
@@ -537,7 +534,7 @@
             part_stream(1, ("y", "zz", "x"), sem + 9),
             part_stream(2, ("zz", "x", "y"), sem + 18),
             last_stream(sem + 27),
-            gather_stream(place, sender, REDUCE_BASE + 50, "zyx", get_lines, False),
+            line_stream,
         ]
     )
     line = jnp.zeros((1, LANES), F32)

time: 74.9 us -> 71.9 us (0.960)
  Pallas kernels: 74.1 us -> 70.6 us
    pallas_call x1, Pallas kernels: 72.8 us -> 69.2 us  [local(): pl.pallas_call(head_kernel, out_shape=(jax.ShapeDtypeStruct((32, LANES),...]
where the time goes in v6:
time: 71.9 us; the launch traced here: 71.2 us
  Pallas kernels  70.6 us (98%)
    pallas_call x1, Pallas kernels, local(): pl.pallas_call(head_kernel, out_shape=(jax.ShapeDtypeStruct((32, LANES),...  69.2 us

profile of v6, /device:TPU:1, one launch (start us, length us, event | category | flops | bytes accessed | tf_op | source)
XLA Modules:
  0.0 71.2 jit_solution(3588991048307748896)
XLA Ops:
  0.6 69.2 %shard_map.104 = (f32[32,128]{1,0:T(8,128)}, f32[1,128]{1,0:T(1,128)}) custom-call(f32[128]{0:T(128)} %targets_ref.1, s32[1,64]{1,0:T(1,128)} %bitcast.13, bf16[128,512]{1,0:T(8,128)(2,1)} %emb_ref.1, f32[64,128]{1,0:T(8,128)} %bitcast.8, f32[64,128]{1,0:T(8,128)} %bitcast.9, f32[64,128]{1,0:T(8,128)} %bitcast.10, f32[64,128]{1,0:T(8,128)} %bitcast.11, ...), custom_call_target="tpu_custom_call" | custom-call | tf_op jit(solution)/shard_map/pallas_call | solution.py:568
  69.9 1.3 %shard_map.105 = (f32[32,128]{1,0:T(8,128)}, f32[1,128]{1,0:T(1,128)}) custom-call(f32[32,128]{1,0:T(8,128)} %get-tuple-element.6.grad_ref, f32[1,128]{1,0:T(1,128)} %get-tuple-element.7.line_ref), custom_call_target="tpu_custom_call" | custom-call | tf_op jit(solution)/shard_map/pallas_call | solution.py:603
